TPU v7x, 32 devices: a whole 2x2x4 slice. The times are simulated.
32 devices in a mesh: comp: 16 (over z, x, core), rows: 2 (over y).
Axes of the slice: x: 2, y: 2, z: 4, core: 2. Of those that a mesh axis runs over, the one named last changes fastest.
Arguments:
- hidden_states: bfloat16 [2, 2, 16, 128, 2560], P('rows', None, 'comp'), may hold values from -6 to 6
- queries: bfloat16 [2, 2, 16, 128, 1280], P('rows', None, 'comp'), may hold values from -900 to 900
- new_keys: bfloat16 [2, 2, 16, 128, 1280], P('rows', None, 'comp'), may hold values from -6 to 6
- new_values: bfloat16 [2, 2, 16, 128, 1280], P('rows', None, 'comp'), may hold values from -6 to 6
- out_grad: bfloat16 [2, 2, 16, 128, 1280], P('rows', None, 'comp'), may hold values from -6 to 6
- gate_weight: bfloat16 [2560, 128], replicated, may hold values from -0.125 to 0.125
- gate_bias: float32 [128], replicated, may hold values from -2 to 6
- prompt_state: float32 [2, 16, 2, 2, 2, 64, 640], P('rows', 'comp'), may hold values from -6 to 6
- owners: int32 [2, 2], P('rows'), may hold values from 0 to 15
- lengths: int32 [2, 2, 16], P('rows', None, 'comp'), may hold values from 32 to 128
- advantage: float32 [2, 2, 16], P('rows', None, 'comp'), may hold values from -4 to 4
Outputs:
- d_queries: bfloat16 [2, 2, 16, 128, 1280], P('rows', None, 'comp')
- d_keys: bfloat16 [2, 2, 16, 128, 1280], P('rows', None, 'comp')
- d_values: bfloat16 [2, 2, 16, 128, 1280], P('rows', None, 'comp')
- d_hidden: bfloat16 [2, 2, 16, 128, 2560], P('rows', None, 'comp')
- d_gate_weight: float32 [2560, 128], replicated
- d_gate_bias: float32 [128], replicated
- d_state: float32 [2, 2, 2, 2, 64, 640], P('rows', None, None, None, 'comp')
All inputs are finite; a program needn't handle non-finite values.
Results may differ from a plain program's by a relative error of at most 0.011.
Values sent between devices are 32-bit elements; how exact they have to be, the bound alone decides.
A program may use at most 64 MiB of HBM per device.

v0:
```python
import jax
import jax.numpy as jnp
from jax import lax
from jax.sharding import PartitionSpec as P


def broadcast(block, axis, holder):
    block = jnp.where(lax.axis_index(axis) == holder, block, jnp.zeros_like(block))
    return lax.psum(block, axis)


def slot_forward(gates, queries, keys_in, values_in, anchor_point):
    steps = queries.shape[0]
    heads = anchor_point.shape[1]
    slots = anchor_point.shape[2]
    width = anchor_point.shape[3]
    highest_score = lax.Precision.HIGHEST
    log_keep = jax.nn.log_sigmoid(gates).reshape(steps, heads, slots) / 8.0
    running = jnp.cumsum(log_keep, axis=0)
    inflow = -jnp.expm1(log_keep)
    places = jnp.arange(steps, dtype=jnp.int32)
    lower = (places[:, None] >= places[None, :])[:, :, None, None]
    between = running[:, None] - running[None, :]
    reach = jnp.where(lower, jnp.exp(jnp.where(lower, between, 0.0)), 0.0) * inflow[None]
    score_scale = width ** (-0.5)
    query_head_count = queries.astype(jnp.float32).reshape(steps, heads, width)
    key_heads = keys_in.astype(jnp.float32).reshape(steps, heads, width)
    value_heads = values_in.astype(jnp.float32).reshape(steps, heads, width)
    pairs = jnp.einsum("thd,jhd->thj", query_head_count, key_heads) * score_scale
    carried_state = jnp.exp(running)
    anchor_score_rows = (
        jnp.einsum("icv,crv->icr", query_head_count, anchor_point[0], precision=highest_score)
        * score_scale
    )
    scores = (
        jnp.einsum("tjhm,thj->thm", reach, pairs, precision=highest_score)
        + carried_state * anchor_score_rows
    )
    slot_probabilities = jax.nn.softmax(scores, axis=-1)
    mixing = jnp.einsum("thm,tjhm->thj", slot_probabilities, reach, precision=highest_score).astype(
        jnp.bfloat16
    )
    result_output = jnp.einsum("thj,jhd->thd", mixing.astype(jnp.float32), value_heads)
    result_output = result_output + jnp.einsum(
        "ivw,vwb->ivb", slot_probabilities * carried_state, anchor_point[1], precision=highest_score
    )
    return result_output.reshape(steps, heads * width)


def shards(
    hidden_states,
    queries,
    new_keys,
    new_values,
    out_grad,
    gate_weight,
    gate_bias,
    prompt_state,
    owners,
    lengths,
    advantage,
):
    local_states = prompt_state[0, 0]
    prompts = local_states.shape[0]
    steps = queries.shape[3]
    received = []
    for prompt in range(prompts):
        received.append(broadcast(local_states[prompt], "comp", owners[0, prompt]))
    anchors = jnp.stack(received)
    places = jnp.arange(steps, dtype=jnp.int32)
    sum_weight = jnp.zeros(gate_weight.shape, jnp.float32)
    sum_bias = jnp.zeros(gate_bias.shape, jnp.float32)
    state_terms = []
    out_q, out_k, out_v, out_x = ([], [], [], [])
    for prompt in range(prompts):
        list_q, list_k, list_v, list_x = ([], [], [], [])
        tokens = hidden_states[0, prompt, 0]
        gates = jnp.dot(tokens, gate_weight, preferred_element_type=jnp.float32) + gate_bias
        live = jnp.where(places < lengths[0, prompt, 0], 1.0, 0.0).astype(jnp.float32)
        cotangent = (advantage[0, prompt, 0] * live)[:, None] * out_grad[0, prompt, 0].astype(
            jnp.float32
        )
        result_output, pullback = jax.vjp(
            slot_forward,
            gates,
            queries[0, prompt, 0],
            new_keys[0, prompt, 0],
            new_values[0, prompt, 0],
            anchors[prompt],
        )
        grad_gates, grad_q, grad_k, grad_v, grad_anchor = pullback(cotangent)
        gates_low = grad_gates.astype(jnp.bfloat16)
        list_x.append(
            jnp.dot(gates_low, gate_weight.T, preferred_element_type=jnp.float32).astype(
                jnp.bfloat16
            )
        )
        sum_weight = sum_weight + jnp.dot(tokens.T, gates_low, preferred_element_type=jnp.float32)
        sum_bias = sum_bias + jnp.sum(grad_gates, axis=0)
        list_q.append(grad_q)
        list_k.append(grad_k)
        list_v.append(grad_v)
        state_terms.append(grad_anchor)
        out_q.append(jnp.stack(list_q))
        out_k.append(jnp.stack(list_k))
        out_v.append(jnp.stack(list_v))
        out_x.append(jnp.stack(list_x))
    state_grads = jnp.stack(state_terms)
    d_state, weight_block, bias_block = (
        lax.psum_scatter(state_grads, "comp", scatter_dimension=3, tiled=True),
        lax.psum_scatter(sum_weight, "comp", scatter_dimension=0, tiled=True),
        lax.psum_scatter(sum_bias, "comp", scatter_dimension=0, tiled=True),
    )
    weight_block, bias_block = lax.psum((weight_block, bias_block), "rows")
    d_weight, d_bias = (
        lax.all_gather(weight_block, "comp", axis=0, tiled=True),
        lax.all_gather(bias_block, "comp", axis=0, tiled=True),
    )
    return (
        jnp.stack(out_q)[None],
        jnp.stack(out_k)[None],
        jnp.stack(out_v)[None],
        jnp.stack(out_x)[None],
        d_weight,
        d_bias,
        d_state[None],
    )


def solution(mesh):
    placed = (
        P("rows", None, "comp", None, None),
        P("rows", None, "comp", None, None),
        P("rows", None, "comp", None, None),
        P("rows", None, "comp", None, None),
        P("rows", None, "comp", None, None),
        P(),
        P(),
        P("rows", "comp", None, None, None, None, None),
        P("rows", None),
        P("rows", None, "comp"),
        P("rows", None, "comp"),
    )
    return jax.shard_map(
        shards,
        mesh=mesh,
        in_specs=placed,
        out_specs=(
            P("rows", None, "comp", None, None),
            P("rows", None, "comp", None, None),
            P("rows", None, "comp", None, None),
            P("rows", None, "comp", None, None),
            P(),
            P(),
            P("rows", None, None, None, "comp", None),
        ),
        check_vma=False,
    )
```

profile of v0, /device:TPU:0, one launch (start us, length us, event | category | flops | bytes accessed | tf_op | source)
XLA Modules:
  0.0 446.6 jit_solution(5496281987982016223)
XLA Ops:
  9.8 2.4 select_bitcast_fusion.1
  31.5 10.2 %fusion.10 = f32[128,2,1,64]{3,2,1,0:T(1,128)} fusion(f32[128,2,64]{0,2,1:T(8,128)} %exponential-minus-one_negate_fusion.1, f32[128,2,64]{0,2,1:T(8,128)S(1)} %copy.149, f32[128,2,64]{2,1,0:T(2,128)} %copy-done.29, pred[128,128]{1,0:T(8,128)(4,1)S(1)} %iota_compare_fusion, bf16[128,2,128,1]{2,0,1,3:T(8,128)(2,1)S(1)} %bitcast.438), kind=kOutput, calls=%fused_computation.19 | convolution fusion | flops 33554432 | bytes 344064 | tf_op jit(solution)/shard_map/transpose(jvp(thm,tjhm->thj))/dot_general | solution.py:40
  41.8 10.8 %multiply_reduce_fusion.3 = (f32[128,2,64]{2,1,0:T(2,128)}, f32[128,2,64]{2,1,0:T(2,128)}) fusion(f32[128,2,128]{2,1,0:T(2,128)S(1)} %copy-done.39, f32[128,2,64]{0,2,1:T(8,128)S(1)} %copy-done.46, f32[128,2,64]{0,2,1:T(8,128)S(1)} %copy.149, f32[128,2,64]{2,1,0:T(2,128)S(1)} %copy-done.30, pred[128,128]{1,0:T(8,128)(4,1)S(1)} %iota_compare_fusion, ...), kind=kLoop, calls=%fused_computation.5 | loop fusion | flops 25133056 | bytes 802816
  56.2 1.6 copy.215
  57.8 1.6 copy.236
  61.1 1.7 copy.191
  62.8 9.9 %fusion.4 = f32[128,2,1,64]{3,2,1,0:T(1,128)} fusion(f32[128,2,64]{0,2,1:T(8,128)} %exponential-minus-one_negate_fusion, f32[128,2,64]{0,2,1:T(8,128)S(1)} %copy.164, f32[128,2,64]{2,1,0:T(2,128)} %copy-done.25, pred[128,128]{1,0:T(8,128)(4,1)S(1)} %iota_compare_fusion, bf16[128,2,128,1]{2,0,1,3:T(8,128)(2,1)} %bitcast.437), kind=kOutput, calls=%fused_computation.14 | convolution fusion | flops 33554432 | bytes 344064 | tf_op jit(solution)/shard_map/transpose(jvp(thm,tjhm->thj))/dot_general | solution.py:40
  74.4 35.2 %all-reduce.16.cloned.1.call-done = (f32[2,2,64,640]{3,2,1,0:T(8,128)}, f32[2,2,64,640]{3,2,1,0:T(8,128)}) async-done(((f32[2,2,64,640]{3,2,1,0:T(8,128)}, f32[2,2,64,640]{3,2,1,0:T(8,128)}), (f32[2,2,64,640]{3,2,1,0:T(8,128)}, f32[2,2,64,640]{3,2,1,0:T(8,128)})) %all-reduce.16.cloned.1.call-update) | async-done | bytes 1310736 | tf_op jit(solution)/shard_map/psum | solution.py:9
  109.5 2.0 fusion.162
  112.1 1.9 fusion.160
  117.5 1.6 copy.267
  120.6 1.6 multiply_reduce_fusion.6
  124.3 1.6 copy.269
  126.7 12.0 %multiply_reduce_fusion.2 = (f32[128,2,128]{2,1,0:T(2,128)}, f32[128,2,128]{2,1,0:T(2,128)}) fusion(f32[128,2,64]{2,1,0:T(2,128)} %copy.267, f32[128,2,64]{0,2,1:T(8,128)} %exponential-minus-one_negate_fusion.1, f32[128,2,64]{0,2,1:T(8,128)S(1)} %copy.149, f32[128,2,64]{2,1,0:T(2,128)} %copy-done.29, pred[128,128]{1,0:T(8,128)(4,1)} %copy-done.48, ...), kind=kLoop, calls=%fused_computation.4 | loop fusion | flops 25100288 | bytes 802816
  138.8 19.8 %fusion.13 = (f32[128,2,64]{0,2,1:T(8,128)}, f32[128,2,64]{2,1,0:T(2,128)}, f32[128,2,64]{0,2,1:T(8,128)}, f32[128,2,64]{0,2,1:T(8,128)}, f32[128,2,64]{2,1,0:T(2,128)}, /*index=5*/f32[128,2,64]{0,2,1:T(8,128)}) fusion(f32[128,2,64]{2,1,0:T(2,128)S(1)} %copy-done.33, f32[128,2,128]{2,1,0:T(2,128)S(1)} %copy-done.40, f32[128,2,64]{2,1,0:T(2,128)S(1)} %copy-done.34, ...), kind=kLoop, calls=%fused_computation.21 | loop fusion | flops 58621952 | bytes 1589248 | tf_op jit(solution)/shard_map/transpose(jvp())/reduce_sum | solution.py:23
  158.6 1.6 copy.188
  160.2 1.7 fusion.132
  161.9 1.6 copy.189
  163.5 2.6 reduce_window_sum.41
  166.0 1.6 copy.190
  170.5 1.6 copy.195
  172.2 1.7 fusion.124
  173.8 1.6 copy.196
  175.4 2.6 reduce_window_sum.43
  178.0 1.6 copy.197
  179.5 1.8 fusion.156
  181.9 31.7 %all-reduce.5 = f32[128]{0:T(128)} all-reduce(f32[128]{0:T(128)} %negate_add_fusion), channel_id=3, replica_groups=mesh['comp'=16,'rows'=2] {'comp'}, use_global_device_ids=true, to_apply=%region_22.24.clone | all-reduce | flops 128 | bytes 1024
  216.5 2.8 copy.256
  221.0 9.9 %fusion.8 = bf16[128,2,1,128]{3,2,1,0:T(2,128)(2,1)} fusion(f32[128,2,64,1]{2,3,1,0:T(1,128)} %copy.248, f32[128,2,64]{0,2,1:T(8,128)} %exponential-minus-one_negate_fusion.1, f32[128,2,64]{0,2,1:T(8,128)S(1)} %copy.149, f32[128,2,64]{2,1,0:T(2,128)} %copy-done.29, pred[128,128]{1,0:T(8,128)(4,1)} %copy-done.48), kind=kOutput, calls=%fused_computation.18 | convolution fusion | flops 33554432 | bytes 344064 | tf_op jit(solution)/shard_map/jvp(thm,tjhm->thj)/dot_general | solution.py:40
  230.9 5.5 %psum.31 = f32[8]{0:T(128)} all-reduce(f32[8]{0:T(128)} %dynamic-slice.2), channel_id=1, replica_groups=mesh['comp'=16,'rows'=2] {'rows'}, use_global_device_ids=true, to_apply=%region_23.25 | all-reduce | flops 8 | bytes 64 | tf_op jit(solution)/shard_map/psum | solution.py:114
  236.4 1.9 convolution_convert_fusion.5
  238.3 1.9 copy.182
  240.9 1.7 copy.222
  242.6 1.9 fusion.41
  244.5 1.9 copy.179
  253.1 1.6 fusion.84
  254.7 20.6 %reduce-scatter.5.cloned.1.call-done = f32[160,128]{1,0:T(8,128)} async-done(((f32[2560,128]{1,0:T(8,128)}), f32[160,128]{1,0:T(8,128)}) %reduce-scatter.5.cloned.1.call-update) | async-done | bytes 81936
  275.2 1.6 copy.257
  276.9 2.2 pad_maximum_fusion
  281.8 1.7 fusion.85
  284.1 14.6 %all-reduce.12.cloned.1.call-done = f32[160,128]{0,1:T(8,128)} async-done(((f32[160,128]{0,1:T(8,128)}), f32[160,128]{0,1:T(8,128)}) %all-reduce.12.cloned.1.call-update) | async-done | bytes 81936 | tf_op jit(solution)/shard_map/psum | solution.py:114
  298.7 1.6 copy.198
  303.2 8.2 %fusion.2 = bf16[128,2,1,128]{3,2,1,0:T(2,128)(2,1)S(1)} fusion(f32[128,2,64,1]{2,3,1,0:T(1,128)S(1)} %copy-done.32, f32[128,2,64]{0,2,1:T(8,128)S(1)} %copy-done.45, f32[128,2,64]{0,2,1:T(8,128)S(1)} %copy.164, f32[128,2,64]{2,1,0:T(2,128)S(1)} %copy-done.28, pred[128,128]{1,0:T(8,128)(4,1)S(1)} %copy-done.50), kind=kOutput, calls=%fused_computation.13 | convolution fusion | flops 33554432 | bytes 344064 | tf_op jit(solution)/shard_map/jvp(thm,tjhm->thj)/dot_general | solution.py:40
  312.2 33.3 %all-reduce.4 = f32[128]{0:T(128)} all-reduce(f32[128]{0:T(128)S(1)} %dynamic-update-slice), channel_id=1, replica_groups=mesh['comp'=16,'rows'=2] {'comp'}, use_global_device_ids=true, to_apply=%add.4 | all-reduce | flops 128 | bytes 1024
  348.6 48.3 %all-reduce.14.cloned.1.call-done = f32[2,2,2,64,640]{4,3,2,1,0:T(8,128)} async-done(((f32[2,2,2,64,640]{4,3,2,1,0:T(8,128)}), f32[2,2,2,64,640]{4,3,2,1,0:T(8,128)}) %all-reduce.14.cloned.1.call-update) | async-done | bytes 1310736
  396.9 1.6 dynamic-slice_bitcast_fusion
  398.4 39.0 %all-gather.2.cloned.1.call-done = f32[2560,128]{1,0:T(8,128)} async-done(((f32[160,128]{1,0:T(8,128)}), f32[2560,128]{1,0:T(8,128)}) %all-gather.2.cloned.1.call-update) | async-done | bytes 1310736 | tf_op jit(solution)/shard_map/all_gather | solution.py:116
  437.4 2.5 copy.288
  (215 shorter events, 59.2 us)
Async XLA Ops:
  7.2 5.2 %copy-start = (bf16[2560,128]{1,0:T(8,128)(2,1)S(1)}, bf16[2560,128]{1,0:T(8,128)(2,1)}, u32[]{:S(2)}) copy-start(bf16[2560,128]{1,0:T(8,128)(2,1)} %param.17) | copy-start | bytes 1966084
  7.2 102.3 %all-reduce.16.cloned.1.call-start = ((), (), s32[]{:S(2)}) async-start(), calls=%async_computation.5 | async-start | bytes 2621440 | tf_op jit(solution)/shard_map/psum | solution.py:9
  12.3 262.9 %reduce-scatter.5.cloned.1.call-start = ((), (), s32[]{:S(2)}) async-start(), calls=%async_computation.3 | async-start | bytes 1392640
  13.6 49.2 %copy-start.48 = (pred[128,128]{1,0:T(8,128)(4,1)}, pred[128,128]{1,0:T(8,128)(4,1)S(1)}, u32[]{:S(2)}) copy-start(pred[128,128]{1,0:T(8,128)(4,1)S(1)} %iota_compare_fusion) | copy-start | bytes 49156
  14.6 2.6 copy-start.57
  14.6 3.2 copy-start.58
  15.4 4.1 copy-start.16
  20.9 2.4 copy-start.18
  23.3 1.8 copy-start.19
  28.9 2.5 copy-start.55
  30.1 22.4 %copy-start.53 = (f32[128]{0:T(128)}, f32[128]{0:T(128)S(1)}, u32[]{:S(2)}) copy-start(f32[128]{0:T(128)S(1)} %fusion.147) | copy-start | bytes 1540
  31.5 10.3 %copy-start.26 = (f32[128,2,64]{2,1,0:T(2,128)S(1)}, f32[128,2,64]{2,1,0:T(2,128)}, u32[]{:S(2)}) copy-start(f32[128,2,64]{2,1,0:T(2,128)} %copy-done.25) | copy-start | bytes 196612
  31.5 10.2 %copy-start.30 = (f32[128,2,64]{2,1,0:T(2,128)S(1)}, f32[128,2,64]{2,1,0:T(2,128)}, u32[]{:S(2)}) copy-start(f32[128,2,64]{2,1,0:T(2,128)} %copy-done.29) | copy-start | bytes 196612
  31.5 10.2 %copy-start.37 = (f32[128,2,128]{2,1,0:T(2,128)S(1)}, f32[128,2,128]{2,1,0:T(2,128)}, u32[]{:S(2)}) copy-start(f32[128,2,128]{2,1,0:T(2,128)} %copy.268) | copy-start | bytes 393220
  31.5 10.2 %copy-start.39 = (f32[128,2,128]{2,1,0:T(2,128)S(1)}, f32[128,2,128]{2,1,0:T(2,128)}, u32[]{:S(2)}) copy-start(f32[128,2,128]{2,1,0:T(2,128)} %copy.266) | copy-start | bytes 393220
  31.5 10.2 %copy-start.43 = (f32[128,2,64]{0,2,1:T(8,128)S(1)}, f32[128,2,64]{0,2,1:T(8,128)}, u32[]{:S(2)}) copy-start(f32[128,2,64]{0,2,1:T(8,128)} %exponential-minus-one_negate_fusion) | copy-start | bytes 196612
  31.5 10.2 %copy-start.46 = (f32[128,2,64]{0,2,1:T(8,128)S(1)}, f32[128,2,64]{0,2,1:T(8,128)}, u32[]{:S(2)}) copy-start(f32[128,2,64]{0,2,1:T(8,128)} %exponential-minus-one_negate_fusion.1) | copy-start | bytes 196612
  41.7 10.8 %copy-start.12 = (bf16[1,1,1,128,1280]{3,4,2,1,0:T(8,128)(2,1)S(1)}, bf16[1,1,1,128,1280]{3,4,2,1,0:T(8,128)(2,1)}, u32[]{:S(2)}) copy-start(bf16[1,1,1,128,1280]{3,4,2,1,0:T(8,128)(2,1)} %copy.263) | copy-start | bytes 983044
  61.1 53.0 %copy-start.3 = (f32[128,2,1,64]{0,3,1,2:T(8,128)}, f32[128,2,1,64]{0,3,1,2:T(8,128)S(1)}, u32[]{:S(2)}) copy-start(f32[128,2,1,64]{0,3,1,2:T(8,128)S(1)} %copy.207) | copy-start | bytes 196612
  73.7 46.9 %copy-start.2 = (f32[128,2,1,64]{0,3,1,2:T(8,128)}, f32[128,2,1,64]{0,3,1,2:T(8,128)S(1)}, u32[]{:S(2)}) copy-start(f32[128,2,1,64]{0,3,1,2:T(8,128)S(1)} %copy.228) | copy-start | bytes 196612
  109.5 4.5 %copy-start.6 = (f32[2,2,64,640]{3,2,1,0:T(8,128)S(1)}, f32[2,2,64,640]{3,2,1,0:T(8,128)}, u32[]{:S(2)}) copy-start(f32[2,2,64,640]{3,2,1,0:T(8,128)} %get-tuple-element.57) | copy-start | bytes 1966084
  111.5 6.0 %copy-start.4 = (f32[128,2,64]{0,2,1:T(8,128)}, f32[128,2,64]{0,2,1:T(8,128)S(1)}, u32[]{:S(2)}) copy-start(f32[128,2,64]{0,2,1:T(8,128)S(1)} %get-tuple-element.65) | copy-start | bytes 196612
  114.0 1.9 copy-start.5
  115.4 2.1 copy-start.14
  126.6 12.1 %copy-start.27 = (f32[128,2,64]{2,1,0:T(2,128)S(1)}, f32[128,2,64]{2,1,0:T(2,128)}, u32[]{:S(2)}) copy-start(f32[128,2,64]{2,1,0:T(2,128)} %copy-done.25) | copy-start | bytes 196612
  126.6 12.1 %copy-start.31 = (f32[128,2,64]{2,1,0:T(2,128)S(1)}, f32[128,2,64]{2,1,0:T(2,128)}, u32[]{:S(2)}) copy-start(f32[128,2,64]{2,1,0:T(2,128)} %copy-done.29) | copy-start | bytes 196612
  126.6 12.1 %copy-start.33 = (f32[128,2,64]{2,1,0:T(2,128)S(1)}, f32[128,2,64]{2,1,0:T(2,128)}, u32[]{:S(2)}) copy-start(f32[128,2,64]{2,1,0:T(2,128)} %copy.267) | copy-start | bytes 196612
  126.6 12.1 %copy-start.34 = (f32[128,2,64]{2,1,0:T(2,128)S(1)}, f32[128,2,64]{2,1,0:T(2,128)}, u32[]{:S(2)}) copy-start(f32[128,2,64]{2,1,0:T(2,128)} %copy.185) | copy-start | bytes 196612
  126.7 12.1 %copy-start.35 = (f32[128,2,64]{2,1,0:T(2,128)S(1)}, f32[128,2,64]{2,1,0:T(2,128)}, u32[]{:S(2)}) copy-start(f32[128,2,64]{2,1,0:T(2,128)} %copy.269) | copy-start | bytes 196612
  126.7 12.1 %copy-start.36 = (f32[128,2,64]{2,1,0:T(2,128)S(1)}, f32[128,2,64]{2,1,0:T(2,128)}, u32[]{:S(2)}) copy-start(f32[128,2,64]{2,1,0:T(2,128)} %copy.192) | copy-start | bytes 196612
  126.7 12.1 %copy-start.38 = (f32[128,2,128]{2,1,0:T(2,128)S(1)}, f32[128,2,128]{2,1,0:T(2,128)}, u32[]{:S(2)}) copy-start(f32[128,2,128]{2,1,0:T(2,128)} %copy.268) | copy-start | bytes 393220
  126.7 12.1 %copy-start.40 = (f32[128,2,128]{2,1,0:T(2,128)S(1)}, f32[128,2,128]{2,1,0:T(2,128)}, u32[]{:S(2)}) copy-start(f32[128,2,128]{2,1,0:T(2,128)} %copy.266) | copy-start | bytes 393220
  126.7 12.1 %copy-start.41 = (f32[128,2,128]{2,1,0:T(2,128)S(1)}, f32[128,2,128]{2,1,0:T(2,128)}, u32[]{:S(2)}) copy-start(f32[128,2,128]{2,1,0:T(2,128)} %copy.184) | copy-start | bytes 393220
  126.7 12.1 %copy-start.42 = (f32[128,2,128]{2,1,0:T(2,128)S(1)}, f32[128,2,128]{2,1,0:T(2,128)}, u32[]{:S(2)}) copy-start(f32[128,2,128]{2,1,0:T(2,128)} %copy.191) | copy-start | bytes 393220
  126.7 12.1 %copy-start.44 = (f32[128,2,64]{0,2,1:T(8,128)S(1)}, f32[128,2,64]{0,2,1:T(8,128)}, u32[]{:S(2)}) copy-start(f32[128,2,64]{0,2,1:T(8,128)} %exponential-minus-one_negate_fusion) | copy-start | bytes 196612
  126.7 12.1 %copy-start.47 = (f32[128,2,64]{0,2,1:T(8,128)S(1)}, f32[128,2,64]{0,2,1:T(8,128)}, u32[]{:S(2)}) copy-start(f32[128,2,64]{0,2,1:T(8,128)} %exponential-minus-one_negate_fusion.1) | copy-start | bytes 196612
  126.7 12.1 %copy-start.49 = (pred[128,128]{1,0:T(8,128)(4,1)S(1)}, pred[128,128]{1,0:T(8,128)(4,1)}, u32[]{:S(2)}) copy-start(pred[128,128]{1,0:T(8,128)(4,1)} %copy-done.48) | copy-start | bytes 49156
  213.6 1.5 copy-start.9
  213.6 1.6 copy-start.22
  219.3 79.4 %all-reduce.12.cloned.1.call-start = ((), (), s32[]{:S(2)}) async-start(), calls=%async_computation.1 | async-start | bytes 262144 | tf_op jit(solution)/shard_map/psum | solution.py:114
  246.3 3.6 copy-start.56
  247.3 3.6 copy-start.54
  276.9 120.0 %all-reduce.14.cloned.1.call-start = ((), (), s32[]{:S(2)}) async-start(), calls=%async_computation.4 | async-start | bytes 2621440
  279.2 2.6 copy-start.21
  279.2 158.2 %all-gather.2.cloned.1.call-start = ((), (), s32[]{:S(2)}) async-start(), calls=%async_computation.2 | async-start | bytes 1392640 | tf_op jit(solution)/shard_map/all_gather | solution.py:116
  300.4 1.6 copy-start.11
  311.4 34.1 %copy-start.24 = (f32[128,128]{0,1:T(8,128)S(1)}, f32[128,128]{0,1:T(8,128)}, u32[]{:S(2)}) copy-start(f32[128,128]{0,1:T(8,128)} %get-tuple-element.59) | copy-start | bytes 196612
  311.4 34.4 %copy-start.23 = (f32[128,128]{0,1:T(8,128)S(1)}, f32[128,128]{0,1:T(8,128)}, u32[]{:S(2)}) copy-start(f32[128,128]{0,1:T(8,128)} %get-tuple-element.107) | copy-start | bytes 196612
  (18 other events, 19.6 us)
Sparse Core Ops, SparseCore 0:
  12.4 97.0 all-reduce.15
  219.4 55.7 reduce-scatter.4
  278.1 20.5 all-reduce.11
  302.6 94.2 all-reduce.13
  399.0 38.3 all-gather.1
where the time goes:
time: 452 us; the launch traced here: 447 us
  waiting for transfers between devices  158 us (35%)
  other arithmetic  76 us (17%)
  blocking collectives  70.6 us (16%)
  matrix products  64.4 us (14%)
  local copies, waits for them, and re-layouts  59.2 us (13%)
  between operations  17.9 us (4%)
    unnamed x7, waiting for transfers between devices  69 us
    unnamed x2, blocking collectives  65 us
    all_gather x1, waiting for transfers between devices, shards(): lax.all_gather(weight_block, 'comp', axis=0, tiled=True)  39 us
    dot_general x4, matrix products, slot_forward(): jnp.einsum('thm,tjhm->thj', slot_probabilities, reach, precision=highest_...  38.2 us
    psum x1, waiting for transfers between devices, broadcast(): return lax.psum(block, axis)  35.2 us
    unnamed x140, local copies, waits for them, and re-layouts  24.1 us
    unnamed x3, other arithmetic  23.9 us
    reduce_sum x1, other arithmetic, slot_forward(): between = running[:, None] - running[None, :]  19.8 us
  transfers between devices with their start and end apart: 5, of which 5 were waited for; matrix products, arithmetic and copies ran while one was open for 24% of the time, Pallas kernels for 0%

commit v1 on v0

v1 whole, which is shorter than its diff:
```python
import functools

import jax
import jax.numpy as jnp
from jax import lax
from jax.experimental import pallas as pl
from jax.experimental.pallas import tpu as pltpu
from jax.sharding import PartitionSpec as P

F32 = jnp.float32
BF16 = jnp.bfloat16
NN = (((1,), (0,)), ((), ()))
NT = (((1,), (1,)), ((), ()))
TN = (((0,), (0,)), ((), ()))


def dot(a, b, dims=NN):
    return lax.dot_general(a, b, dims, preferred_element_type=F32)


def dot_full(a, b, dims=NN):
    return lax.dot_general(
        a, b, dims, precision=lax.Precision.HIGHEST, preferred_element_type=F32
    )


def pieces(x, count):
    out = []
    for _ in range(count):
        top = x.astype(BF16)
        out.append(top)
        x = x - top.astype(F32)
    return out


def mix_kernel(
    lengths_ref, advantage_ref, x_ref, q_ref, k_ref, v_ref, og_ref, w_ref, bias_ref, anchor_ref,
    dq_ref, dk_ref, dv_ref, dx_ref, dw_ref, db_ref, ds_ref,
    decay_ref, flow_ref, mix_ref, pair_ref, *, chunk,
):
    prompt = pl.program_id(0)
    steps = x_ref.shape[1]
    heads, slots, width = anchor_ref.shape[2:]
    lanes = heads * slots
    blocks = steps // chunk
    scale = width ** (-0.5)
    lane = lax.broadcasted_iota(jnp.int32, (1, lanes), 1)
    of_head = [(lane >= h * slots) & (lane < (h + 1) * slots) for h in range(heads)]
    row = lax.broadcasted_iota(jnp.int32, (steps, 1), 0)
    column = lax.broadcasted_iota(jnp.int32, (1, steps), 1)
    local = lax.broadcasted_iota(jnp.int32, (chunk, 1), 0)
    lower = jnp.where(row >= column, 1.0, 0.0).astype(BF16)

    def by_head(parts):
        out = parts[-1]
        for h in range(heads - 2, -1, -1):
            out = jnp.where(lane < (h + 1) * slots, parts[h], out)
        return out

    def head_reduce(x, op):
        return by_head(
            [op(x[:, h * slots:(h + 1) * slots], axis=1, keepdims=True) for h in range(heads)]
        )

    def head(ref, h):
        return ref[0, :, h * width:(h + 1) * width]

    x = x_ref[0]
    w = w_ref[...]
    gates = dot(x, w) + bias_ref[...]
    small = jnp.exp(-jnp.abs(gates))
    one = 1.0 + small
    gap = one - 1.0
    log_one = jnp.where(gap == 0.0, small, jnp.log(one) * (small / jnp.where(gap == 0.0, 1.0, gap)))
    keep = -(jnp.maximum(-gates, 0.0) + log_one) / 8.0
    down = jnp.where(gates >= 0.0, small, 1.0) / one
    kept = jnp.exp(keep)
    series = jnp.ones_like(keep)
    for degree in range(9, 1, -1):
        series = 1.0 + keep * series * (1.0 / degree)
    inflow = jnp.where(keep > -0.5, -keep * series, 1.0 - kept)
    cum = sum(dot(lower, part) for part in pieces(keep, 3))
    carried = jnp.exp(cum)

    live = jnp.where(row < lengths_ref[prompt], advantage_ref[prompt], 0.0)
    qk, dm, seen, back = [], [], [], []
    for h in range(heads):
        q, og = head(q_ref, h), head(og_ref, h)
        qk.append(dot(q, head(k_ref, h), NT) * scale)
        dm.append(dot(og, head(v_ref, h), NT) * live)
        seen.append(sum(dot(q, part, NT) for part in pieces(anchor_ref[0, 0, h], 3)))
        back.append(sum(dot(og, part, NT) for part in pieces(anchor_ref[0, 1, h], 3)))
    seen = jnp.concatenate(seen, axis=1) * (scale * carried)
    back = jnp.concatenate(back, axis=1) * (live * carried)

    def block_rows(b):
        rows = slice(b * chunk, (b + 1) * chunk)
        return jnp.concatenate([part for h in range(heads) for part in (qk[h][rows], dm[h][rows])])

    def before(b):
        start = cum[b * chunk - 1:b * chunk]
        far = jnp.where(row < b * chunk, jnp.exp(start - cum), 0.0)
        near = jnp.exp(cum[b * chunk:(b + 1) * chunk] - start)
        return far, near

    def columns(parts, rows, at):
        return by_head([part[rows, at:at + 1] for part in parts])

    scores, d_probs = [], []
    for b in range(blocks):
        rows = slice(b * chunk, (b + 1) * chunk)
        score, d_prob = seen[rows], back[rows]
        for j in range(chunk):
            at = b * chunk + j
            decay = jnp.where(local >= j, jnp.exp(cum[rows] - cum[at:at + 1]), 0.0)
            decay_ref[at] = decay
            reach = decay * inflow[at:at + 1]
            score = score + reach * columns(qk, rows, at)
            d_prob = d_prob + reach * columns(dm, rows, at)
        if b:
            far, near = before(b)
            got = dot_full(block_rows(b), far * inflow)
            got = [got[i * chunk:(i + 1) * chunk] for i in range(2 * heads)]
            score = score + near * by_head(got[0::2])
            d_prob = d_prob + near * by_head(got[1::2])
        scores.append(score)
        d_probs.append(d_prob)
    scores = jnp.concatenate(scores)
    d_probs = jnp.concatenate(d_probs)
    probs = jnp.exp(scores - head_reduce(scores, jnp.max))
    probs = probs / head_reduce(probs, jnp.sum)
    weighted = probs * d_probs
    d_scores = probs * (d_probs - head_reduce(weighted, jnp.sum))

    flow_ref[...] = jnp.zeros_like(flow_ref)
    for b in range(blocks):
        rows = slice(b * chunk, (b + 1) * chunk)
        mix = [jnp.zeros((chunk, steps), F32)] * heads
        pair = [jnp.zeros((chunk, steps), F32)] * heads
        if b:
            far, near = before(b)
            left = [probs[rows] * near, d_scores[rows] * near]
            left = jnp.concatenate(
                [jnp.where(mine, part, 0.0) for mine in of_head for part in (left[1], left[0])]
            )
            got = dot_full(left, far * inflow, NT)
            for h in range(heads):
                pair[h] = got[2 * h * chunk:(2 * h + 1) * chunk]
                mix[h] = got[(2 * h + 1) * chunk:(2 * h + 2) * chunk]
            flow_ref[...] += far * dot_full(block_rows(b), left, TN)
        for j in range(chunk):
            at = b * chunk + j
            decay = decay_ref[at]
            up, down_part = decay * probs[rows], decay * d_scores[rows]
            flow_ref[at:at + 1] += jnp.sum(
                up * columns(dm, rows, at) + down_part * columns(qk, rows, at),
                axis=0, keepdims=True,
            )
            up, down_part = up * inflow[at:at + 1], down_part * inflow[at:at + 1]
            for h in range(heads):
                part = slice(h * slots, (h + 1) * slots)
                here = column == at
                mix[h] = jnp.where(here, jnp.sum(up[:, part], axis=1, keepdims=True), mix[h])
                pair[h] = jnp.where(
                    here, jnp.sum(down_part[:, part], axis=1, keepdims=True), pair[h]
                )
        for h in range(heads):
            mix_ref[h, rows] = mix[h]
            pair_ref[h, rows] = pair[h]

    from_scores = d_scores * carried * scale
    from_probs = probs * carried * live
    for h in range(heads):
        part = slice(h * slots, (h + 1) * slots)
        at = slice(h * width, (h + 1) * width)
        q, og = head(q_ref, h), head(og_ref, h)
        pair = (pair_ref[h] * scale).astype(BF16)
        state_high, state_low = pieces(from_scores[:, part], 2)
        key_high, key_low = pieces(anchor_ref[0, 0, h], 2)
        d_q = dot(pair, head(k_ref, h)) + dot(state_high, key_high)
        d_q = d_q + dot(state_high, key_low) + dot(state_low, key_high)
        dq_ref[0, :, at] = d_q.astype(BF16)
        dk_ref[0, :, at] = dot(pair, q, TN).astype(BF16)
        cotangent = (og.astype(F32) * live).astype(BF16)
        dv_ref[0, :, at] = dot(mix_ref[h].astype(BF16), cotangent, TN).astype(BF16)
        ds_ref[0, 0, h] = dot(state_high, q, TN) + dot(state_low, q, TN)
        high, low = pieces(from_probs[:, part], 2)
        ds_ref[0, 1, h] = dot(high, og, TN) + dot(low, og, TN)

    flow = flow_ref[...]
    d_cum = weighted + d_scores * scores - flow * inflow
    d_keep = sum(dot(lower, part, TN) for part in pieces(d_cum, 3)) - flow * kept
    d_gates = d_keep * down * 0.125
    low = d_gates.astype(BF16)
    dx_ref[0] = dot(low, w, NT).astype(BF16)
    d_w = dot(x, low, TN)
    d_b = jnp.sum(d_gates, axis=0, keepdims=True)

    @pl.when(prompt == 0)
    def _():
        dw_ref[...] = d_w
        db_ref[...] = d_b

    @pl.when(prompt > 0)
    def _():
        dw_ref[...] += d_w
        db_ref[...] += d_b


def local_grads(x, q, k, v, og, weight, bias, anchors, lengths, advantage, interpret=False):
    prompts, steps, depth = x.shape
    inner = q.shape[2]
    lanes = weight.shape[1]
    heads = anchors.shape[2]
    chunk = 16

    def per_prompt(a):
        shape = (1,) + a.shape[1:]
        return pl.BlockSpec(shape, lambda p: (p,) + (0,) * (len(shape) - 1))

    def whole(shape):
        return pl.BlockSpec(shape, lambda p: (0,) * len(shape))

    smem = pl.BlockSpec(memory_space=pltpu.SMEM)
    shapes = (
        jax.ShapeDtypeStruct(q.shape, BF16),
        jax.ShapeDtypeStruct(q.shape, BF16),
        jax.ShapeDtypeStruct(q.shape, BF16),
        jax.ShapeDtypeStruct(x.shape, BF16),
        jax.ShapeDtypeStruct(weight.shape, F32),
        jax.ShapeDtypeStruct((1, lanes), F32),
        jax.ShapeDtypeStruct(anchors.shape, F32),
    )
    return pl.pallas_call(
        functools.partial(mix_kernel, chunk=chunk),
        grid=(prompts,),
        out_shape=shapes,
        in_specs=[smem, smem] + [per_prompt(a) for a in (x, q, k, v, og)]
        + [whole(weight.shape), whole((1, lanes)), per_prompt(anchors)],
        out_specs=tuple(per_prompt(s) for s in shapes[:4])
        + (whole(weight.shape), whole((1, lanes)), per_prompt(anchors)),
        scratch_shapes=[
            pltpu.VMEM((steps, chunk, lanes), F32),
            pltpu.VMEM((steps, lanes), F32),
            pltpu.VMEM((heads, steps, steps), F32),
            pltpu.VMEM((heads, steps, steps), F32),
        ],
        compiler_params=pltpu.CompilerParams(
            dimension_semantics=("arbitrary",), vmem_limit_bytes=48 * 2**20
        ),
        interpret=interpret,
    )(lengths, advantage, x, q, k, v, og, weight, bias.reshape(1, lanes), anchors)


def shards(
    hidden_states, queries, new_keys, new_values, out_grad, gate_weight, gate_bias,
    prompt_state, owners, lengths, advantage,
):
    me = lax.axis_index("comp")
    mine = (owners[0] == me)[:, None, None, None, None]
    anchors = lax.psum(jnp.where(mine, prompt_state[0, 0], 0.0), "comp")
    dq, dk, dv, dx, d_weight, d_bias, d_state = local_grads(
        hidden_states[0, :, 0], queries[0, :, 0], new_keys[0, :, 0], new_values[0, :, 0],
        out_grad[0, :, 0], gate_weight, gate_bias, anchors, lengths[0, :, 0], advantage[0, :, 0],
    )
    d_state = lax.psum_scatter(d_state, "comp", scatter_dimension=3, tiled=True)
    block = lax.psum_scatter(d_weight, "comp", scatter_dimension=0, tiled=True)
    block = lax.psum(block, "rows")
    d_weight = lax.all_gather(block, "comp", axis=0, tiled=True)
    d_bias = lax.psum(d_bias, ("comp", "rows"))[0]
    return (
        dq[None, :, None], dk[None, :, None], dv[None, :, None], dx[None, :, None],
        d_weight, d_bias, d_state[None],
    )


def solution(mesh):
    tokens = P("rows", None, "comp", None, None)
    return jax.shard_map(
        shards,
        mesh=mesh,
        in_specs=(
            tokens, tokens, tokens, tokens, tokens, P(), P(),
            P("rows", "comp", None, None, None, None, None),
            P("rows", None), P("rows", None, "comp"), P("rows", None, "comp"),
        ),
        out_specs=(
            tokens, tokens, tokens, tokens, P(), P(),
            P("rows", None, None, None, "comp", None),
        ),
        check_vma=False,
    )
```

time: 452 us -> 384 us (0.85); the launches traced: 447 us -> 383 us
  waiting for transfers between devices: 158 us -> 275 us
  other arithmetic: 76 us -> 3.33 us
  matrix products: 64.4 us -> 0 us
  local copies, waits for them, and re-layouts: 59.2 us -> 4.65 us
  Pallas kernels: 0 us -> 46.4 us
  blocking collectives: 70.6 us -> 39.4 us
    psum x2, waiting for transfers between devices: 49.8 us -> 120 us  [the longest x1 98.2 us: shards(): anchors = lax.psum(jnp.where(mine, prompt_state[0, 0], 0.0), 'comp')]
    unnamed x2 -> x0, blocking collectives: 65 us -> none
    dot_general x30 -> x0, matrix products: 64.4 us -> none  [the longest x4 38.2 us: slot_forward(): jnp.einsum('thm,tjhm->thj', slot_probabilities, reach, precision=highest_...]
    reduce_scatter x0 -> x1, waiting for transfers between devices: none -> 58.4 us  [shards(): block = lax.psum_scatter(d_weight, 'comp', scatter_dimension=0, tiled=True)]
    pallas_call x0 -> x1, Pallas kernels: none -> 46.4 us  [local_grads(): pl.pallas_call(functools.partial(mix_kernel, chunk=chunk), grid=(prompts,...]
    psum x1, blocking collectives: 5.53 us -> 39.4 us  [shards(): d_bias = lax.psum(d_bias, ('comp', 'rows'))[0]]
    unnamed x3 -> x0, other arithmetic: 23.9 us -> none
    reduce_sum x4 -> x0, other arithmetic: 21.7 us -> none  [the longest x1 19.8 us: slot_forward(): between = running[:, None] - running[None, :]]
  transfers between devices with their start and end apart: 5 -> 5, of which waited for: 5 -> 5; matrix products, arithmetic and copies ran while one was open for 24% -> 1% of each run, Pallas kernels for 0% -> 0%
where the time goes in v1:
time: 384 us; the launch traced here: 383 us
  waiting for transfers between devices  275 us (72%)
  Pallas kernels  46.4 us (12%)
  blocking collectives  39.4 us (10%)
  between operations  14.5 us (4%)
  local copies, waits for them, and re-layouts  4.65 us (1%)
    psum x1, waiting for transfers between devices, shards(): anchors = lax.psum(jnp.where(mine, prompt_state[0, 0], 0.0), 'comp')  98.2 us
    reduce_scatter x1, waiting for transfers between devices, shards(): block = lax.psum_scatter(d_weight, 'comp', scatter_dimension=0, tiled=True)  58.4 us
    unnamed x6, waiting for transfers between devices  57.7 us
    pallas_call x1, Pallas kernels, local_grads(): pl.pallas_call(functools.partial(mix_kernel, chunk=chunk), grid=(prompts,...  46.4 us
    psum x1, blocking collectives, shards(): d_bias = lax.psum(d_bias, ('comp', 'rows'))[0]  39.4 us
    all_gather x1, waiting for transfers between devices, shards(): d_weight = lax.all_gather(block, 'comp', axis=0, tiled=True)  39 us
    psum x1, waiting for transfers between devices, shards(): block = lax.psum(block, 'rows')  21.7 us
  transfers between devices with their start and end apart: 5, of which 5 were waited for; matrix products, arithmetic and copies ran while one was open for 1% of the time, Pallas kernels for 0%

profile of v1, /device:TPU:0, one launch (start us, length us, event | category | flops | bytes accessed | tf_op | source)
XLA Modules:
  0.0 383.4 jit_solution(6707626440233489109)
XLA Ops:
  7.2 0.0 all-reduce.5.cloned.1.call-start
  7.2 0.7 compare_bitcast_fusion
  7.9 0.0 copy-start.2
  7.9 0.0 copy-start.3
  7.9 0.0 copy-start.4
  7.9 2.7 bitcast_select_fusion
  10.6 0.0 copy-start
  10.6 0.0 copy-start.1
  10.6 0.0 copy-start.5
  10.6 0.0 copy-start.6
  10.6 0.0 copy-start.7
  10.6 0.0 all-reduce.5.cloned.1.call-update
  10.6 0.0 reduce-scatter.3.cloned.1.call-start
  10.7 98.2 %all-reduce.5.cloned.1.call-done.anchor_ref = f32[2,2,2,64,640]{4,3,2,1,0:T(8,128)} async-done(((f32[2,2,2,64,640]{4,3,2,1,0:T(8,128)}), f32[2,2,2,64,640]{4,3,2,1,0:T(8,128)}) %all-reduce.5.cloned.1.call-update) | async-done | bytes 1310736 | tf_op jit(solution)/shard_map/psum | solution.py:261
  108.8 0.0 copy-done.2
  108.8 0.0 copy-done.3
  108.8 0.0 copy-done.4
  108.8 0.0 copy-done
  108.8 0.0 copy-done.1
  108.9 0.0 copy-done.5
  108.9 0.0 copy-done.6
  108.9 0.0 copy-done.7
  108.9 46.4 %shard_map.162 = (bf16[2,128,1280]{2,1,0:T(8,128)(2,1)}, bf16[2,128,1280]{2,1,0:T(8,128)(2,1)}, bf16[2,128,1280]{2,1,0:T(8,128)(2,1)}, bf16[2,128,2560]{2,1,0:T(...) custom-call(s32[2]{0:T(128)S(1)} %bitcast.34, f32[2]{0:T(128)S(1)} %bitcast.35, ...), custom_call_target="tpu_custom_call" | custom-call | tf_op jit(solution)/shard_map/pallas_call | solution.py:234
  155.2 0.0 copy-start.8
  155.3 0.0 reduce-scatter.3.cloned.1.call-update
  155.3 0.0 all-reduce.7.cloned.1.call-start
  155.3 58.4 %reduce-scatter.3.cloned.1.call-done = f32[160,128]{1,0:T(8,128)} async-done(((f32[2560,128]{1,0:T(8,128)}), f32[160,128]{1,0:T(8,128)}) %reduce-scatter.3.cloned.1.call-update) | async-done | bytes 81936 | tf_op jit(solution)/shard_map/reduce_scatter | solution.py:267
  213.8 0.0 all-reduce.7.cloned.1.call-update
  213.8 0.0 all-reduce.9.cloned.1.call-start
  213.8 0.5 all-reduce.9.cloned.1.call-update
  214.4 0.0 all-gather.2.cloned.1.call-start
  214.4 21.7 %all-reduce.7.cloned.1.call-done = f32[160,128]{1,0:T(8,128)} async-done(((f32[160,128]{1,0:T(8,128)}), f32[160,128]{1,0:T(8,128)}) %all-reduce.7.cloned.1.call-update) | async-done | bytes 81936 | tf_op jit(solution)/shard_map/psum | solution.py:268
  236.1 0.0 all-gather.2.cloned.1.call-update
  236.1 0.0 copy-done.8
  236.1 0.6 dynamic-slice
  237.4 39.4 %psum.23 = f32[128]{0:T(128)} all-reduce(f32[128]{0:T(128)S(1)} %bitcast.37), channel_id=1, replica_groups=mesh['comp'=16,'rows'=2] {'comp','rows'}, use_global_device_ids=true, to_apply=%region_3.4 | all-reduce | flops 128 | bytes 1024 | tf_op jit(solution)/shard_map/psum | solution.py:270
  276.8 57.1 %all-reduce.9.cloned.1.call-done = f32[2,2,2,64,640]{4,3,2,1,0:T(8,128)} async-done(((f32[2,2,2,64,640]{4,3,2,1,0:T(8,128)}), f32[2,2,2,64,640]{4,3,2,1,0:T(8,128)}) %all-reduce.9.cloned.1.call-update) | async-done | bytes 1310736
  333.9 1.6 dynamic-slice_bitcast_fusion
  335.5 39.0 %all-gather.2.cloned.1.call-done = f32[2560,128]{1,0:T(8,128)} async-done(((f32[160,128]{1,0:T(8,128)}), f32[2560,128]{1,0:T(8,128)}) %all-gather.2.cloned.1.call-update) | async-done | bytes 1310736 | tf_op jit(solution)/shard_map/all_gather | solution.py:269
  374.4 2.5 copy.32
Async XLA Ops:
  7.2 101.7 %all-reduce.5.cloned.1.call-start = ((), (), s32[]{:S(2)}) async-start(), calls=%async_computation.1 | async-start | bytes 2621440 | tf_op jit(solution)/shard_map/psum | solution.py:261
  7.9 101.0 %copy-start.2 = (bf16[1,2,1,128,1280]{4,3,2,1,0:T(8,128)(2,1)S(1)}, bf16[1,2,1,128,1280]{4,3,2,1,0:T(8,128)(2,1)}, u32[]{:S(2)}) copy-start(bf16[1,2,1,128,1280]{4,3,2,1,0:T(8,128)(2,1)} %param.14) | copy-start | bytes 1966084
  7.9 101.0 %copy-start.3 = (bf16[1,2,1,128,1280]{4,3,2,1,0:T(8,128)(2,1)S(1)}, bf16[1,2,1,128,1280]{4,3,2,1,0:T(8,128)(2,1)}, u32[]{:S(2)}) copy-start(bf16[1,2,1,128,1280]{4,3,2,1,0:T(8,128)(2,1)} %param.15) | copy-start | bytes 1966084
  7.9 101.0 %copy-start.4 = (bf16[2560,128]{1,0:T(8,128)(2,1)S(1)}, bf16[2560,128]{1,0:T(8,128)(2,1)}, u32[]{:S(2)}) copy-start(bf16[2560,128]{1,0:T(8,128)(2,1)} %w_ref.1) | copy-start | bytes 1966084
  10.6 98.3 %copy-start = (bf16[1,2,1,128,1280]{4,3,2,1,0:T(8,128)(2,1)S(1)}, bf16[1,2,1,128,1280]{4,3,2,1,0:T(8,128)(2,1)}, u32[]{:S(2)}) copy-start(bf16[1,2,1,128,1280]{4,3,2,1,0:T(8,128)(2,1)} %param.12) | copy-start | bytes 1966084
  10.6 98.3 %copy-start.1 = (bf16[1,2,1,128,1280]{4,3,2,1,0:T(8,128)(2,1)S(1)}, bf16[1,2,1,128,1280]{4,3,2,1,0:T(8,128)(2,1)}, u32[]{:S(2)}) copy-start(bf16[1,2,1,128,1280]{4,3,2,1,0:T(8,128)(2,1)} %param.13) | copy-start | bytes 1966084
  10.6 98.3 %copy-start.5 = (s32[1,2,1]{1,2,0:T(1,128)S(1)}, s32[1,2,1]{1,2,0:T(1,128)}, u32[]{:S(2)}) copy-start(s32[1,2,1]{1,2,0:T(1,128)} %param.20) | copy-start | bytes 28
  10.6 98.3 %copy-start.6 = (f32[1,2,1]{1,2,0:T(1,128)S(1)}, f32[1,2,1]{1,2,0:T(1,128)}, u32[]{:S(2)}) copy-start(f32[1,2,1]{1,2,0:T(1,128)} %param.21) | copy-start | bytes 28
  10.6 98.3 %copy-start.7 = (f32[128]{0:T(128)S(1)}, f32[128]{0:T(128)}, u32[]{:S(2)}) copy-start(f32[128]{0:T(128)} %param.17) | copy-start | bytes 1540
  10.6 203.2 %reduce-scatter.3.cloned.1.call-start = ((), (), s32[]{:S(2)}) async-start(), calls=%async_computation.2 | async-start | bytes 1392640 | tf_op jit(solution)/shard_map/reduce_scatter | solution.py:267
  155.2 80.9 %copy-start.8 = (u32[32]{0:T(128)S(1)}, u32[32]{0:T(128)}, u32[]{:S(2)}) copy-start(u32[32]{0:T(128)} %constant.19) | copy-start | bytes 388
  155.3 80.8 %all-reduce.7.cloned.1.call-start = ((), (), s32[]{:S(2)}) async-start(), calls=%async_computation.3 | async-start | bytes 163840 | tf_op jit(solution)/shard_map/psum | solution.py:268
  213.8 120.1 %all-reduce.9.cloned.1.call-start = ((), (), s32[]{:S(2)}) async-start(), calls=%async_computation.5 | async-start | bytes 2621440
  214.4 160.1 %all-gather.2.cloned.1.call-start = ((), (), s32[]{:S(2)}) async-start(), calls=%async_computation.4 | async-start | bytes 1392640 | tf_op jit(solution)/shard_map/all_gather | solution.py:269
Sparse Core Ops, SparseCore 0:
  12.0 96.7 all-reduce.4
  155.4 58.3 reduce-scatter.2
  216.0 20.0 all-reduce.6
  239.4 94.4 all-reduce.8
  336.0 38.3 all-gather.1

commit v2 on v1

--- a/solution.py
+++ b/solution.py
@@ -252,32 +252,223 @@
     )(lengths, advantage, x, q, k, v, og, weight, bias.reshape(1, lanes), anchors)
 
 
+class Stream:
+    def __init__(self, axis, bits, source, rows, held, sems, row_axis=None, row_bits=0,
+                 row_held=None, gathered=None):
+        me = lax.axis_index(axis)
+        self.axis, self.bits, self.source, self.rows, self.held = axis, bits, source, rows, held
+        self.send_sem, self.recv_sem = sems
+        self.row_axis, self.row_bits, self.row_held = row_axis, row_bits, row_held
+        self.gathered = gathered
+        self.mine = [me // 2 ** bit % 2 for bit in range(bits)]
+        self.partner = [me + (1 - 2 * self.mine[bit]) * 2 ** bit for bit in range(bits)]
+        if row_bits:
+            row = lax.axis_index(row_axis)
+            self.row_partner = [row + (1 - 2 * (row // 2 ** b % 2)) * 2 ** b for b in range(row_bits)]
+        self.steps = bits + row_bits + (bits if gathered is not None else 0)
+        self.copies = []
+
+    def start(self, src, dst, axis, partner):
+        step = len(self.copies)
+        copy = pltpu.make_async_remote_copy(
+            src_ref=src, dst_ref=dst, send_sem=self.send_sem.at[step],
+            recv_sem=self.recv_sem.at[step], device_id={axis: partner},
+            device_id_type=pl.DeviceIdType.MESH,
+        )
+        copy.start()
+        self.copies.append(copy)
+
+    def side(self, step, bit_value):
+        free = self.bits - 1 - step
+        index = (slice(None),) * free + (bit_value,)
+        if step == 0:
+            return self.source, index + (self.rows,)
+        return self.held[step - 1], index
+
+    def total(self):
+        return self.row_held[-1] if self.row_bits else self.held[-1]
+
+    def begin(self, step):
+        if step < self.bits:
+            ref, index = self.side(step, 1 - self.mine[step])
+            self.start(ref.at[index], self.held[step], self.axis, self.partner[step])
+            return
+        step -= self.bits
+        if step < self.row_bits:
+            ref = self.row_held[step - 1] if step else self.held[-1]
+            self.start(ref, self.row_held[step], self.row_axis, self.row_partner[step])
+            return
+        step -= self.row_bits
+        if step == 0:
+            own = tuple(self.mine[::-1]) + (self.rows,)
+            self.gathered[own] = self.total()[...]
+        bit = self.bits - 1 - step
+        index = (slice(None),) * step + tuple(self.mine[bit::-1]) + (self.rows,)
+        ref = self.gathered.at[index]
+        self.start(ref, ref, self.axis, self.partner[bit])
+
+    def end(self, step):
+        self.copies[step].wait_recv()
+        if step < self.bits:
+            ref, index = self.side(step, self.mine[step])
+            self.held[step][...] += ref[index]
+        elif step < self.bits + self.row_bits:
+            step -= self.bits
+            ref = self.row_held[step - 1] if step else self.held[-1]
+            self.row_held[step][...] += ref[...]
+
+    def drain(self):
+        for copy in self.copies:
+            copy.wait_send()
+
+
+def greet(axes):
+    barrier = pltpu.get_barrier_semaphore()
+    count = 0
+    for axis, bits in axes:
+        me = lax.axis_index(axis)
+        for bit in range(bits):
+            other = me + (1 - 2 * (me // 2 ** bit % 2)) * 2 ** bit
+            pl.semaphore_signal(
+                barrier, inc=1, device_id={axis: other}, device_id_type=pl.DeviceIdType.MESH
+            )
+            count += 1
+    pl.semaphore_wait(barrier, count)
+
+
+def run(streams, delays):
+    last = max(s.steps + d for s, d in zip(streams, delays))
+    for time in range(last + 1):
+        for stream, delay in zip(streams, delays):
+            step = time - delay
+            if 1 <= step <= stream.steps:
+                stream.end(step - 1)
+            if 0 <= step < stream.steps:
+                stream.begin(step)
+    for stream in streams:
+        stream.drain()
+
+
+def halves(bits, rows, columns):
+    return [
+        pltpu.VMEM((2,) * (bits - 1 - step) + (rows, columns), F32) for step in range(bits)
+    ]
+
+
+def split_rows(rows, parts):
+    each = -(-rows // parts // 8) * 8
+    return [slice(at, min(at + each, rows)) for at in range(0, rows, each)]
+
+
+def sum_everywhere(blocks, bits):
+    rows, columns = blocks.shape[-2:]
+    pieces_of = split_rows(rows, 2)
+    count = len(pieces_of)
+
+    def kernel(x_ref, o_ref, *scratch):
+        streams = []
+        for i, part in enumerate(pieces_of):
+            own = scratch[i * (bits + 2):(i + 1) * (bits + 2)]
+            streams.append(Stream("comp", bits, x_ref, part, own[:bits], own[bits:], gathered=o_ref))
+        greet([("comp", bits)])
+        run(streams, list(range(count)))
+
+    scratch = []
+    for part in pieces_of:
+        scratch += halves(bits, part.stop - part.start, columns)
+        scratch += [pltpu.SemaphoreType.DMA((2 * bits,))] * 2
+    vmem = pl.BlockSpec(memory_space=pltpu.VMEM)
+    return pl.pallas_call(
+        kernel,
+        out_shape=jax.ShapeDtypeStruct(blocks.shape, F32),
+        in_specs=[vmem],
+        out_specs=vmem,
+        scratch_shapes=scratch,
+        compiler_params=pltpu.CompilerParams(collective_id=0, has_side_effects=True),
+    )(blocks)
+
+
+def reduce_all(state, weight, bits, row_bits):
+    rows, columns = state.shape[-2:]
+    w_rows, w_columns = weight.shape[-2:]
+    parts = split_rows(rows, 2)
+
+    def kernel(s_ref, w_ref, so_ref, wo_ref, *scratch):
+        w_scratch, rest = scratch[:bits + row_bits + 2], scratch[bits + row_bits + 2:]
+        streams = [Stream(
+            "comp", bits, w_ref, slice(None), w_scratch[:bits], w_scratch[-2:], row_axis="rows",
+            row_bits=row_bits, row_held=w_scratch[bits:bits + row_bits], gathered=wo_ref,
+        )]
+        for i, part in enumerate(parts):
+            own = rest[i * (bits + 2):(i + 1) * (bits + 2)]
+            streams.append(Stream("comp", bits, s_ref, part, own[:bits], own[bits:]))
+        greet([("comp", bits), ("rows", row_bits)])
+        run(streams, list(range(len(streams))))
+        for stream in streams[1:]:
+            so_ref[stream.rows] = stream.total()[...]
+
+    scratch = halves(bits, w_rows, w_columns)
+    scratch += [pltpu.VMEM((w_rows, w_columns), F32)] * row_bits
+    scratch += [pltpu.SemaphoreType.DMA((2 * bits + row_bits,))] * 2
+    for part in parts:
+        scratch += halves(bits, part.stop - part.start, columns)
+        scratch += [pltpu.SemaphoreType.DMA((bits,))] * 2
+    vmem = pl.BlockSpec(memory_space=pltpu.VMEM)
+    return pl.pallas_call(
+        kernel,
+        out_shape=(
+            jax.ShapeDtypeStruct((rows, columns), F32),
+            jax.ShapeDtypeStruct(weight.shape, F32),
+        ),
+        in_specs=[vmem, vmem],
+        out_specs=(vmem, vmem),
+        scratch_shapes=scratch,
+        compiler_params=pltpu.CompilerParams(collective_id=1, has_side_effects=True),
+    )(state, weight)
+
+
+def log2(count):
+    return count.bit_length() - 1
+
+
 def shards(
-    hidden_states, queries, new_keys, new_values, out_grad, gate_weight, gate_bias,
+    comp, rows, hidden_states, queries, new_keys, new_values, out_grad, gate_weight, gate_bias,
     prompt_state, owners, lengths, advantage,
 ):
+    bits, row_bits = log2(comp), log2(rows)
+    cube = (2,) * bits
+    local = prompt_state[0, 0]
     me = lax.axis_index("comp")
     mine = (owners[0] == me)[:, None, None, None, None]
-    anchors = lax.psum(jnp.where(mine, prompt_state[0, 0], 0.0), "comp")
+    width = local.shape[-1]
+    anchors = sum_everywhere(jnp.where(mine, local, 0.0).reshape(cube + (-1, width)), bits)
     dq, dk, dv, dx, d_weight, d_bias, d_state = local_grads(
         hidden_states[0, :, 0], queries[0, :, 0], new_keys[0, :, 0], new_values[0, :, 0],
-        out_grad[0, :, 0], gate_weight, gate_bias, anchors, lengths[0, :, 0], advantage[0, :, 0],
-    )
-    d_state = lax.psum_scatter(d_state, "comp", scatter_dimension=3, tiled=True)
-    block = lax.psum_scatter(d_weight, "comp", scatter_dimension=0, tiled=True)
-    block = lax.psum(block, "rows")
-    d_weight = lax.all_gather(block, "comp", axis=0, tiled=True)
-    d_bias = lax.psum(d_bias, ("comp", "rows"))[0]
+        out_grad[0, :, 0], gate_weight, gate_bias, anchors.reshape(local.shape),
+        lengths[0, :, 0], advantage[0, :, 0],
+    )
+    prompts, kinds, heads, slots, _ = local.shape
+    own = slots // comp
+    state = d_state.reshape(prompts * kinds * heads, comp, own, width).transpose(1, 0, 2, 3)
+    lanes = gate_weight.shape[1]
+    weight = jnp.concatenate(
+        [d_weight.reshape(comp, -1, lanes), jnp.broadcast_to(d_bias, (comp, 8, lanes))], axis=1
+    )
+    state, weight = reduce_all(
+        state.reshape(cube + (-1, width)), weight.reshape(cube + weight.shape[1:]), bits, row_bits
+    )
+    weight = weight.reshape((comp,) + weight.shape[-2:])
     return (
         dq[None, :, None], dk[None, :, None], dv[None, :, None], dx[None, :, None],
-        d_weight, d_bias, d_state[None],
+        weight[:, :-8].reshape(gate_weight.shape), weight[0, -1],
+        state.reshape(1, prompts, kinds, heads, own, width),
     )
 
 
 def solution(mesh):
     tokens = P("rows", None, "comp", None, None)
     return jax.shard_map(
-        shards,
+        functools.partial(shards, mesh.shape["comp"], mesh.shape["rows"]),
         mesh=mesh,
         in_specs=(
             tokens, tokens, tokens, tokens, tokens, P(), P(),

time: 384 us -> 148 us (0.39)
  waiting for transfers between devices: 275 us -> 0 us
  Pallas kernels: 46.4 us -> 134 us
  blocking collectives: 39.4 us -> 0 us
  between operations: 14.5 us -> 0.75 us
  local copies, waits for them, and re-layouts: 4.65 us -> 8.62 us
    psum x2 -> x0, waiting for transfers between devices: 120 us -> none  [the longest x1 98.2 us: shards(): anchors = lax.psum(jnp.where(mine, prompt_state[0, 0], 0.0), 'comp')]
    pallas_call x0 -> x2, Pallas kernels: none -> 88.5 us  [the longest x1 49.1 us: reduce_all(): pl.pallas_call(kernel, out_shape=(jax.ShapeDtypeStruct((rows, columns), F...]
    reduce_scatter x1 -> x0, waiting for transfers between devices: 58.4 us -> none  [shards(): block = lax.psum_scatter(d_weight, 'comp', scatter_dimension=0, tiled=True)]
    unnamed x6 -> x0, waiting for transfers between devices: 57.7 us -> none
    psum x1 -> x0, blocking collectives: 39.4 us -> none  [shards(): d_bias = lax.psum(d_bias, ('comp', 'rows'))[0]]
    all_gather x1 -> x0, waiting for transfers between devices: 39 us -> none  [shards(): d_weight = lax.all_gather(block, 'comp', axis=0, tiled=True)]
  transfers between devices with their start and end apart: 5 -> 0, of which waited for: 5 -> 0; matrix products, arithmetic and copies ran while one was open for 1% -> 0% of each run, Pallas kernels for 0% -> 0%
where the time goes in v2:
time: 148 us
  Pallas kernels  134 us (91%)
  local copies, waits for them, and re-layouts  8.62 us (6%)
  other arithmetic  4.43 us (3%)
    pallas_call x1, Pallas kernels, reduce_all(): pl.pallas_call(kernel, out_shape=(jax.ShapeDtypeStruct((rows, columns), F...  49.1 us
    pallas_call x1, Pallas kernels, local_grads(): pl.pallas_call(functools.partial(mix_kernel, chunk=chunk), grid=(prompts,...  45.6 us
    pallas_call x1, Pallas kernels, sum_everywhere(): pl.pallas_call(kernel, out_shape=jax.ShapeDtypeStruct(blocks.shape, F32),...  39.3 us

profile of v2, /device:TPU:0, one launch (start us, length us, event | category | flops | bytes accessed | tf_op | source)
XLA Modules:
  0.0 147.9 jit_solution(11919701893957640641)
XLA Ops:
  0.6 0.7 compare_bitcast_fusion
  1.3 2.6 %broadcast_select_fusion.x_ref = f32[2,2,2,2,32,640]{5,4,3,2,1,0:T(8,128)} fusion(f32[2,2,2,2,32,640]{5,4,3,2,1,0:T(8,128)} %bitcast.48, pred[2]{0:T(512)(128)(4,1)S(1)} %compare_bitcast_fusion), kind=kLoop, calls=%fused_computation.2 | loop fusion | flops 327680 | bytes 2621442 | tf_op jit(solution)/shard_map/jit(_where)/select_n | solution.py:444
  3.9 0.0 copy-start
  3.9 0.0 copy-start.1
  3.9 0.0 copy-start.2
  3.9 0.0 copy-start.5
  3.9 0.0 copy-start.6
  3.9 0.0 copy-start.7
  3.9 39.3 %shard_map.162 = f32[2,2,2,2,32,640]{5,4,3,2,1,0:T(8,128)} custom-call(f32[2,2,2,2,32,640]{5,4,3,2,1,0:T(8,128)} %broadcast_select_fusion.x_ref), custom_call_target="tpu_custom_call" | custom-call | tf_op jit(solution)/shard_map/pallas_call | solution.py:381
  43.2 0.0 copy-done
  43.2 0.0 copy-done.1
  43.2 0.0 copy-done.2
  43.3 0.0 copy-done.5
  43.3 0.0 copy-done.6
  43.3 0.0 copy-done.7
  43.3 0.0 copy-start.3
  43.3 1.1 copy-done.3
  44.4 0.0 copy-start.4
  44.4 1.1 copy-done.4
  45.5 45.6 %shard_map.163 = (bf16[2,128,1280]{2,1,0:T(8,128)(2,1)}, bf16[2,128,1280]{2,1,0:T(8,128)(2,1)}, bf16[2,128,1280]{2,1,0:T(8,128)(2,1)}, bf16[2,128,2560]{2,1,0:T(...) custom-call(s32[2]{0:T(128)S(1)} %bitcast.40, f32[2]{0:T(128)S(1)} %bitcast.41, ...), custom_call_target="tpu_custom_call" | custom-call | tf_op jit(solution)/shard_map/pallas_call | solution.py:234
  91.1 1.2 pad_maximum_fusion.w_ref
  92.3 0.4 reshape.52
  92.7 0.2 copy.24
  92.9 1.5 %reshape.53.s_ref = f32[2,2,2,2,32,640]{5,4,3,2,1,0:T(8,128)} reshape(f32[16,8,4,640]{3,2,1,0:T(4,128)S(1)} %bitcast.45) | data formatting | bytes 2621440 | tf_op jit(solution)/shard_map/reshape | solution.py:458
  94.4 49.1 %shard_map.164 = (f32[32,640]{1,0:T(8,128)}, f32[2,2,2,2,168,128]{5,4,3,2,1,0:T(8,128)}) custom-call(f32[2,2,2,2,32,640]{5,4,3,2,1,0:T(8,128)} %reshape.53.s_ref, f32[2,2,2,2,168,128]{5,4,3,2,1,0:T(8,128)} %pad_maximum_fusion.w_ref), custom_call_target="tpu_custom_call" | custom-call | tf_op jit(solution)/shard_map/pallas_call | solution.py:417
  143.5 1.2 slice_bitcast_fusion
  144.7 0.0 copy-start.8
  144.7 2.5 %slice.8 = f32[16,160,128]{2,1,0:T(8,128)} slice(f32[16,168,128]{2,1,0:T(8,128)} %bitcast.50), slice={[0:16], [0:160], [0:128]} | slice | bytes 2621440 | tf_op jit(solution)/shard_map/slice | solution.py:463
  147.2 0.0 copy-done.8
  147.2 0.7 reshape.56
  (1 shorter events, 0.0 us)
Async XLA Ops:
  3.9 39.4 %copy-start = (bf16[1,2,1,128,1280]{4,3,2,1,0:T(8,128)(2,1)S(1)}, bf16[1,2,1,128,1280]{4,3,2,1,0:T(8,128)(2,1)}, u32[]{:S(2)}) copy-start(bf16[1,2,1,128,1280]{4,3,2,1,0:T(8,128)(2,1)} %param.12) | copy-start | bytes 1966084
  3.9 39.4 %copy-start.1 = (bf16[1,2,1,128,1280]{4,3,2,1,0:T(8,128)(2,1)S(1)}, bf16[1,2,1,128,1280]{4,3,2,1,0:T(8,128)(2,1)}, u32[]{:S(2)}) copy-start(bf16[1,2,1,128,1280]{4,3,2,1,0:T(8,128)(2,1)} %param.13) | copy-start | bytes 1966084
  3.9 39.4 %copy-start.2 = (bf16[1,2,1,128,1280]{4,3,2,1,0:T(8,128)(2,1)S(1)}, bf16[1,2,1,128,1280]{4,3,2,1,0:T(8,128)(2,1)}, u32[]{:S(2)}) copy-start(bf16[1,2,1,128,1280]{4,3,2,1,0:T(8,128)(2,1)} %param.14) | copy-start | bytes 1966084
  3.9 39.4 %copy-start.5 = (s32[1,2,1]{1,2,0:T(1,128)S(1)}, s32[1,2,1]{1,2,0:T(1,128)}, u32[]{:S(2)}) copy-start(s32[1,2,1]{1,2,0:T(1,128)} %param.20) | copy-start | bytes 28
  3.9 39.4 %copy-start.6 = (f32[1,2,1]{1,2,0:T(1,128)S(1)}, f32[1,2,1]{1,2,0:T(1,128)}, u32[]{:S(2)}) copy-start(f32[1,2,1]{1,2,0:T(1,128)} %param.21) | copy-start | bytes 28
  3.9 39.4 %copy-start.7 = (f32[128]{0:T(128)S(1)}, f32[128]{0:T(128)}, u32[]{:S(2)}) copy-start(f32[128]{0:T(128)} %param.17) | copy-start | bytes 1540
  43.3 1.1 copy-start.3
  44.4 1.1 copy-start.4
  144.7 2.5 %copy-start.8 = (f32[32,640]{1,0:T(8,128)S(1)}, f32[32,640]{1,0:T(8,128)}, u32[]{:S(2)}) copy-start(f32[32,640]{1,0:T(8,128)} %get-tuple-element.24) | copy-start | bytes 245764

commit v3 on v2

--- a/solution.py
+++ b/solution.py
@@ -18,9 +18,15 @@
     return lax.dot_general(a, b, dims, preferred_element_type=F32)
 
 
-def dot_full(a, b, dims=NN):
-    return lax.dot_general(
-        a, b, dims, precision=lax.Precision.HIGHEST, preferred_element_type=F32
+def dot_full(a, b, dims=NN, products=6):
+    (a_axis,), (b_axis,) = dims[0]
+    count = 3 if products == 6 else 2
+    a, b = pieces(a, count), pieces(b, count)
+    terms = [(0, 0), (0, 1), (1, 0), (1, 1), (0, 2), (2, 0)][:products][::-1]
+    return dot(
+        jnp.concatenate([a[i] for i, _ in terms], axis=a_axis),
+        jnp.concatenate([b[j] for _, j in terms], axis=b_axis),
+        dims,
     )
 
 
@@ -35,8 +41,8 @@
 
 def mix_kernel(
     lengths_ref, advantage_ref, x_ref, q_ref, k_ref, v_ref, og_ref, w_ref, bias_ref, anchor_ref,
-    dq_ref, dk_ref, dv_ref, dx_ref, dw_ref, db_ref, ds_ref,
-    decay_ref, flow_ref, mix_ref, pair_ref, *, chunk,
+    dq_ref, dk_ref, dv_ref, dx_ref, dw_ref, ds_ref,
+    decay_ref, mix_ref, pair_ref, *, chunk,
 ):
     prompt = pl.program_id(0)
     steps = x_ref.shape[1]
@@ -48,7 +54,6 @@
     of_head = [(lane >= h * slots) & (lane < (h + 1) * slots) for h in range(heads)]
     row = lax.broadcasted_iota(jnp.int32, (steps, 1), 0)
     column = lax.broadcasted_iota(jnp.int32, (1, steps), 1)
-    local = lax.broadcasted_iota(jnp.int32, (chunk, 1), 0)
     lower = jnp.where(row >= column, 1.0, 0.0).astype(BF16)
 
     def by_head(parts):
@@ -103,70 +108,84 @@
         near = jnp.exp(cum[b * chunk:(b + 1) * chunk] - start)
         return far, near
 
-    def columns(parts, rows, at):
-        return by_head([part[rows, at:at + 1] for part in parts])
-
-    scores, d_probs = [], []
-    for b in range(blocks):
-        rows = slice(b * chunk, (b + 1) * chunk)
-        score, d_prob = seen[rows], back[rows]
-        for j in range(chunk):
-            at = b * chunk + j
-            decay = jnp.where(local >= j, jnp.exp(cum[rows] - cum[at:at + 1]), 0.0)
-            decay_ref[at] = decay
-            reach = decay * inflow[at:at + 1]
-            score = score + reach * columns(qk, rows, at)
-            d_prob = d_prob + reach * columns(dm, rows, at)
-        if b:
-            far, near = before(b)
-            got = dot_full(block_rows(b), far * inflow)
-            got = [got[i * chunk:(i + 1) * chunk] for i in range(2 * heads)]
-            score = score + near * by_head(got[0::2])
-            d_prob = d_prob + near * by_head(got[1::2])
-        scores.append(score)
-        d_probs.append(d_prob)
-    scores = jnp.concatenate(scores)
-    d_probs = jnp.concatenate(d_probs)
+    tiles = (blocks, chunk, lanes)
+    shift = chunk.bit_length() - 1
+    same_block = row >> shift == column >> shift
+    pair_row = lax.broadcasted_iota(jnp.int32, (heads * steps, 1), 0)
+    pair_lane = lax.broadcasted_iota(jnp.int32, (1, chunk * lanes), 1)
+    spread = [
+        jnp.where(
+            ((pair_row[:steps] & (chunk - 1)) == pair_lane >> (lanes.bit_length() - 1))
+            & ((pair_lane & (lanes - 1)) >> (slots.bit_length() - 1) == h), 1.0, 0.0,
+        ).astype(BF16)
+        for h in range(heads)
+    ]
+    spread = jnp.concatenate(spread)
+
+    def near_pairs(parts):
+        kept_pairs = jnp.concatenate([jnp.where(same_block, part, 0.0) for part in parts], axis=1)
+        return sum(dot(part, spread) for part in pieces(kept_pairs, 3))
+
+    def near_sums(parts):
+        got = sum(dot(part, spread, NT) for part in pieces(jnp.concatenate(parts, axis=1), 2))
+        return [jnp.where(same_block, got[:, h * steps:(h + 1) * steps], 0.0) for h in range(heads)]
+
+    def at_place(x, j):
+        x = x.reshape(tiles)[:, j:j + 1]
+        return jnp.broadcast_to(x, tiles).reshape(steps, lanes)
+
+    place = row & (chunk - 1)
+    qk_near, dm_near = near_pairs(qk), near_pairs(dm)
+    scores, d_probs = seen, back
+    for j in range(chunk):
+        part = slice(j * lanes, (j + 1) * lanes)
+        decay = jnp.where(place >= j, jnp.exp(cum - at_place(cum, j)), 0.0)
+        decay_ref[j] = decay
+        reach = decay * at_place(inflow, j)
+        scores = scores + reach * qk_near[:, part]
+        d_probs = d_probs + reach * dm_near[:, part]
+    far_scores = [jnp.zeros((chunk, lanes), F32)]
+    far_probs = [jnp.zeros((chunk, lanes), F32)]
+    for b in range(1, blocks):
+        far, near = before(b)
+        got = dot_full(block_rows(b), far * inflow)
+        got = [got[i * chunk:(i + 1) * chunk] for i in range(2 * heads)]
+        far_scores.append(near * by_head(got[0::2]))
+        far_probs.append(near * by_head(got[1::2]))
+    scores = scores + jnp.concatenate(far_scores)
+    d_probs = d_probs + jnp.concatenate(far_probs)
     probs = jnp.exp(scores - head_reduce(scores, jnp.max))
     probs = probs / head_reduce(probs, jnp.sum)
     weighted = probs * d_probs
     d_scores = probs * (d_probs - head_reduce(weighted, jnp.sum))
 
-    flow_ref[...] = jnp.zeros_like(flow_ref)
-    for b in range(blocks):
+    flow = jnp.zeros((steps, lanes), F32)
+    ups, downs = [], []
+    for j in range(chunk):
+        part = slice(j * lanes, (j + 1) * lanes)
+        decay = decay_ref[j]
+        up, away = decay * probs, decay * d_scores
+        total = (up * dm_near[:, part] + away * qk_near[:, part]).reshape(tiles)
+        total = jnp.broadcast_to(jnp.sum(total, axis=1, keepdims=True), tiles)
+        flow = jnp.where(place == j, total.reshape(steps, lanes), flow)
+        ups.append(up * at_place(inflow, j))
+        downs.append(away * at_place(inflow, j))
+    mix_near, pair_near = near_sums(ups), near_sums(downs)
+    for h in range(heads):
+        mix_ref[h] = mix_near[h]
+        pair_ref[h] = pair_near[h]
+    for b in range(1, blocks):
         rows = slice(b * chunk, (b + 1) * chunk)
-        mix = [jnp.zeros((chunk, steps), F32)] * heads
-        pair = [jnp.zeros((chunk, steps), F32)] * heads
-        if b:
-            far, near = before(b)
-            left = [probs[rows] * near, d_scores[rows] * near]
-            left = jnp.concatenate(
-                [jnp.where(mine, part, 0.0) for mine in of_head for part in (left[1], left[0])]
-            )
-            got = dot_full(left, far * inflow, NT)
-            for h in range(heads):
-                pair[h] = got[2 * h * chunk:(2 * h + 1) * chunk]
-                mix[h] = got[(2 * h + 1) * chunk:(2 * h + 2) * chunk]
-            flow_ref[...] += far * dot_full(block_rows(b), left, TN)
-        for j in range(chunk):
-            at = b * chunk + j
-            decay = decay_ref[at]
-            up, down_part = decay * probs[rows], decay * d_scores[rows]
-            flow_ref[at:at + 1] += jnp.sum(
-                up * columns(dm, rows, at) + down_part * columns(qk, rows, at),
-                axis=0, keepdims=True,
-            )
-            up, down_part = up * inflow[at:at + 1], down_part * inflow[at:at + 1]
-            for h in range(heads):
-                part = slice(h * slots, (h + 1) * slots)
-                here = column == at
-                mix[h] = jnp.where(here, jnp.sum(up[:, part], axis=1, keepdims=True), mix[h])
-                pair[h] = jnp.where(
-                    here, jnp.sum(down_part[:, part], axis=1, keepdims=True), pair[h]
-                )
+        far, near = before(b)
+        left = [d_scores[rows] * near, probs[rows] * near]
+        left = jnp.concatenate(
+            [jnp.where(mine, part, 0.0) for mine in of_head for part in left]
+        )
+        got = dot_full(left, far * inflow, NT, 3)
         for h in range(heads):
-            mix_ref[h, rows] = mix[h]
-            pair_ref[h, rows] = pair[h]
+            pair_ref[h, rows] += got[2 * h * chunk:(2 * h + 1) * chunk]
+            mix_ref[h, rows] += got[(2 * h + 1) * chunk:(2 * h + 2) * chunk]
+        flow = flow + far * dot_full(block_rows(b), left, TN)
 
     from_scores = d_scores * carried * scale
     from_probs = probs * carried * live
@@ -187,7 +206,6 @@
         high, low = pieces(from_probs[:, part], 2)
         ds_ref[0, 1, h] = dot(high, og, TN) + dot(low, og, TN)
 
-    flow = flow_ref[...]
     d_cum = weighted + d_scores * scores - flow * inflow
     d_keep = sum(dot(lower, part, TN) for part in pieces(d_cum, 3)) - flow * kept
     d_gates = d_keep * down * 0.125
@@ -196,23 +214,24 @@
     d_w = dot(x, low, TN)
     d_b = jnp.sum(d_gates, axis=0, keepdims=True)
 
+    d_b = jnp.broadcast_to(d_b, (8, lanes))
+    count = dw_ref.shape[1] - 8
+
     @pl.when(prompt == 0)
     def _():
-        dw_ref[...] = d_w
-        db_ref[...] = d_b
-
-    @pl.when(prompt > 0)
-    def _():
-        dw_ref[...] += d_w
-        db_ref[...] += d_b
-
-
-def local_grads(x, q, k, v, og, weight, bias, anchors, lengths, advantage, interpret=False):
+        dw_ref[...] = jnp.zeros_like(dw_ref)
+
+    for c in range(dw_ref.shape[0]):
+        dw_ref[c, :count] += d_w[c * count:(c + 1) * count]
+        dw_ref[c, count:] += d_b
+
+
+def local_grads(comp, x, q, k, v, og, weight, bias, anchors, lengths, advantage, chunk=8, interpret=False):
     prompts, steps, depth = x.shape
     inner = q.shape[2]
     lanes = weight.shape[1]
     heads = anchors.shape[2]
-    chunk = 16
+    gate_shape = (comp, depth // comp + 8, lanes)
 
     def per_prompt(a):
         shape = (1,) + a.shape[1:]
@@ -227,8 +246,7 @@
         jax.ShapeDtypeStruct(q.shape, BF16),
         jax.ShapeDtypeStruct(q.shape, BF16),
         jax.ShapeDtypeStruct(x.shape, BF16),
-        jax.ShapeDtypeStruct(weight.shape, F32),
-        jax.ShapeDtypeStruct((1, lanes), F32),
+        jax.ShapeDtypeStruct(gate_shape, F32),
         jax.ShapeDtypeStruct(anchors.shape, F32),
     )
     return pl.pallas_call(
@@ -238,10 +256,9 @@
         in_specs=[smem, smem] + [per_prompt(a) for a in (x, q, k, v, og)]
         + [whole(weight.shape), whole((1, lanes)), per_prompt(anchors)],
         out_specs=tuple(per_prompt(s) for s in shapes[:4])
-        + (whole(weight.shape), whole((1, lanes)), per_prompt(anchors)),
+        + (whole(gate_shape), per_prompt(anchors)),
         scratch_shapes=[
-            pltpu.VMEM((steps, chunk, lanes), F32),
-            pltpu.VMEM((steps, lanes), F32),
+            pltpu.VMEM((chunk, steps, lanes), F32),
             pltpu.VMEM((heads, steps, steps), F32),
             pltpu.VMEM((heads, steps, steps), F32),
         ],
@@ -362,7 +379,7 @@
 
 def sum_everywhere(blocks, bits):
     rows, columns = blocks.shape[-2:]
-    pieces_of = split_rows(rows, 2)
+    pieces_of = split_rows(rows, 4)
     count = len(pieces_of)
 
     def kernel(x_ref, o_ref, *scratch):
@@ -391,25 +408,30 @@
 def reduce_all(state, weight, bits, row_bits):
     rows, columns = state.shape[-2:]
     w_rows, w_columns = weight.shape[-2:]
-    parts = split_rows(rows, 2)
+    parts = split_rows(rows, 4)
+    w_parts = split_rows(w_rows, 2)
 
     def kernel(s_ref, w_ref, so_ref, wo_ref, *scratch):
-        w_scratch, rest = scratch[:bits + row_bits + 2], scratch[bits + row_bits + 2:]
-        streams = [Stream(
-            "comp", bits, w_ref, slice(None), w_scratch[:bits], w_scratch[-2:], row_axis="rows",
-            row_bits=row_bits, row_held=w_scratch[bits:bits + row_bits], gathered=wo_ref,
-        )]
-        for i, part in enumerate(parts):
-            own = rest[i * (bits + 2):(i + 1) * (bits + 2)]
+        streams = []
+        for part in w_parts:
+            own, scratch = scratch[:bits + row_bits + 2], scratch[bits + row_bits + 2:]
+            streams.append(Stream(
+                "comp", bits, w_ref, part, own[:bits], own[-2:], row_axis="rows",
+                row_bits=row_bits, row_held=own[bits:bits + row_bits], gathered=wo_ref,
+            ))
+        for part in parts:
+            own, scratch = scratch[:bits + 2], scratch[bits + 2:]
             streams.append(Stream("comp", bits, s_ref, part, own[:bits], own[bits:]))
         greet([("comp", bits), ("rows", row_bits)])
         run(streams, list(range(len(streams))))
-        for stream in streams[1:]:
+        for stream in streams[len(w_parts):]:
             so_ref[stream.rows] = stream.total()[...]
 
-    scratch = halves(bits, w_rows, w_columns)
-    scratch += [pltpu.VMEM((w_rows, w_columns), F32)] * row_bits
-    scratch += [pltpu.SemaphoreType.DMA((2 * bits + row_bits,))] * 2
+    scratch = []
+    for part in w_parts:
+        scratch += halves(bits, part.stop - part.start, w_columns)
+        scratch += [pltpu.VMEM((part.stop - part.start, w_columns), F32)] * row_bits
+        scratch += [pltpu.SemaphoreType.DMA((2 * bits + row_bits,))] * 2
     for part in parts:
         scratch += halves(bits, part.stop - part.start, columns)
         scratch += [pltpu.SemaphoreType.DMA((bits,))] * 2
@@ -442,18 +464,14 @@
     mine = (owners[0] == me)[:, None, None, None, None]
     width = local.shape[-1]
     anchors = sum_everywhere(jnp.where(mine, local, 0.0).reshape(cube + (-1, width)), bits)
-    dq, dk, dv, dx, d_weight, d_bias, d_state = local_grads(
-        hidden_states[0, :, 0], queries[0, :, 0], new_keys[0, :, 0], new_values[0, :, 0],
+    dq, dk, dv, dx, weight, d_state = local_grads(
+        comp, hidden_states[0, :, 0], queries[0, :, 0], new_keys[0, :, 0], new_values[0, :, 0],
         out_grad[0, :, 0], gate_weight, gate_bias, anchors.reshape(local.shape),
         lengths[0, :, 0], advantage[0, :, 0],
     )
     prompts, kinds, heads, slots, _ = local.shape
     own = slots // comp
     state = d_state.reshape(prompts * kinds * heads, comp, own, width).transpose(1, 0, 2, 3)
-    lanes = gate_weight.shape[1]
-    weight = jnp.concatenate(
-        [d_weight.reshape(comp, -1, lanes), jnp.broadcast_to(d_bias, (comp, 8, lanes))], axis=1
-    )
     state, weight = reduce_all(
         state.reshape(cube + (-1, width)), weight.reshape(cube + weight.shape[1:]), bits, row_bits
     )

time: 148 us -> 112 us (0.76)
  Pallas kernels: 134 us -> 97 us
  local copies, waits for them, and re-layouts: 8.62 us -> 10.8 us
    pallas_call x1, Pallas kernels: 45.6 us -> 13.9 us  [local_grads(): pl.pallas_call(functools.partial(mix_kernel, chunk=chunk), grid=(prompts,...]
    pallas_call x1, Pallas kernels: 49.1 us -> 42.1 us  [reduce_all(): pl.pallas_call(kernel, out_shape=(jax.ShapeDtypeStruct((rows, columns), F...]
    unnamed x18 -> x20, local copies, waits for them, and re-layouts: 2.2 us -> 4.37 us
    pallas_call x1, Pallas kernels: 39.3 us -> 41 us  [sum_everywhere(): pl.pallas_call(kernel, out_shape=jax.ShapeDtypeStruct(blocks.shape, F32),...]
where the time goes in v3:
time: 112 us
  Pallas kernels  97 us (87%)
  local copies, waits for them, and re-layouts  10.8 us (10%)
  other arithmetic  3.23 us (3%)
    pallas_call x1, Pallas kernels, reduce_all(): pl.pallas_call(kernel, out_shape=(jax.ShapeDtypeStruct((rows, columns), F...  42.1 us
    pallas_call x1, Pallas kernels, sum_everywhere(): pl.pallas_call(kernel, out_shape=jax.ShapeDtypeStruct(blocks.shape, F32),...  41 us
    pallas_call x1, Pallas kernels, local_grads(): pl.pallas_call(functools.partial(mix_kernel, chunk=chunk), grid=(prompts,...  13.9 us
    unnamed x20, local copies, waits for them, and re-layouts  4.37 us
    select_n x1, other arithmetic, shards(): jnp.where(mine, local, 0.0).reshape(cube + (-1, width))  2.57 us
    slice x1, local copies, waits for them, and re-layouts, shards(): weight[:, :-8].reshape(gate_weight.shape)  2.5 us

profile of v3, /device:TPU:0, one launch (start us, length us, event | category | flops | bytes accessed | tf_op | source)
XLA Modules:
  0.0 111.7 jit_solution(2001628682393366563)
XLA Ops:
  0.6 0.7 compare_bitcast_fusion
  1.3 2.6 %broadcast_select_fusion.x_ref = f32[2,2,2,2,32,640]{5,4,3,2,1,0:T(8,128)} fusion(f32[2,2,2,2,32,640]{5,4,3,2,1,0:T(8,128)} %bitcast.46, pred[2]{0:T(512)(128)(4,1)S(1)} %compare_bitcast_fusion), kind=kLoop, calls=%fused_computation.1 | loop fusion | flops 327680 | bytes 2621442 | tf_op jit(solution)/shard_map/jit(_where)/select_n | solution.py:466
  3.9 0.0 copy-start
  3.9 0.0 copy-start.1
  3.9 0.0 copy-start.6
  3.9 0.0 copy-start.7
  3.9 0.0 copy-start.8
  3.9 41.0 %shard_map.162 = f32[2,2,2,2,32,640]{5,4,3,2,1,0:T(8,128)} custom-call(f32[2,2,2,2,32,640]{5,4,3,2,1,0:T(8,128)} %broadcast_select_fusion.x_ref), custom_call_target="tpu_custom_call" | custom-call | tf_op jit(solution)/shard_map/pallas_call | solution.py:398
  44.9 0.0 copy-done
  44.9 0.0 copy-done.1
  44.9 0.0 copy-done.6
  44.9 0.0 copy-done.7
  44.9 0.0 copy-done.8
  44.9 0.0 copy-start.2
  45.0 1.1 copy-done.2
  46.0 0.0 copy-start.3
  46.0 1.1 copy-done.3
  47.1 0.0 copy-start.4
  47.1 1.1 copy-done.4
  48.2 0.0 copy-start.5
  48.2 1.1 copy-done.5
  49.3 13.9 %shard_map.163 = (bf16[2,128,1280]{2,1,0:T(8,128)(2,1)}, bf16[2,128,1280]{2,1,0:T(8,128)(2,1)}, bf16[2,128,1280]{2,1,0:T(8,128)(2,1)}, bf16[2,128,2560]{2,1,0:T(...) custom-call(s32[2]{0:T(128)S(1)} %bitcast.39, f32[2]{0:T(128)S(1)} %bitcast.40, ...), custom_call_target="tpu_custom_call" | custom-call | tf_op jit(solution)/shard_map/pallas_call | solution.py:252
  63.2 0.4 reshape.49
  63.6 0.2 copy.24
  63.8 1.5 %reshape.50.s_ref = f32[2,2,2,2,32,640]{5,4,3,2,1,0:T(8,128)} reshape(f32[16,8,4,640]{3,2,1,0:T(4,128)S(1)} %bitcast.43) | data formatting | bytes 2621440 | tf_op jit(solution)/shard_map/reshape | solution.py:476
  65.3 42.1 %shard_map.164 = (f32[32,640]{1,0:T(8,128)}, f32[2,2,2,2,168,128]{5,4,3,2,1,0:T(8,128)}) custom-call(f32[2,2,2,2,32,640]{5,4,3,2,1,0:T(8,128)} %reshape.50.s_ref, f32[2,2,2,2,168,128]{5,4,3,2,1,0:T(8,128)} %bitcast.44), custom_call_target="tpu_custom_call" | custom-call | tf_op jit(solution)/shard_map/pallas_call | solution.py:439
  107.4 1.2 %slice_bitcast_fusion = f32[128]{0:T(128)} fusion(f32[16,168,128]{2,1,0:T(8,128)} %bitcast.47), kind=kLoop, calls=%fused_computation.3 | loop fusion | bytes 1024 | tf_op jit(solution)/shard_map/squeeze | solution.py:481
  108.6 0.0 copy-start.9
  108.6 2.5 %slice.8 = f32[16,160,128]{2,1,0:T(8,128)} slice(f32[16,168,128]{2,1,0:T(8,128)} %bitcast.48), slice={[0:16], [0:160], [0:128]} | slice | bytes 2621440 | tf_op jit(solution)/shard_map/slice | solution.py:481
  111.1 0.0 copy-done.9
  111.1 0.7 reshape.54
Async XLA Ops:
  3.9 41.0 %copy-start = (bf16[1,2,1,128,2560]{4,3,2,1,0:T(8,128)(2,1)S(1)}, bf16[1,2,1,128,2560]{4,3,2,1,0:T(8,128)(2,1)}, u32[]{:S(2)}) copy-start(bf16[1,2,1,128,2560]{4,3,2,1,0:T(8,128)(2,1)} %param.11) | copy-start | bytes 3932164
  3.9 41.0 %copy-start.1 = (bf16[1,2,1,128,1280]{4,3,2,1,0:T(8,128)(2,1)S(1)}, bf16[1,2,1,128,1280]{4,3,2,1,0:T(8,128)(2,1)}, u32[]{:S(2)}) copy-start(bf16[1,2,1,128,1280]{4,3,2,1,0:T(8,128)(2,1)} %param.12) | copy-start | bytes 1966084
  3.9 41.1 %copy-start.6 = (s32[1,2,1]{1,2,0:T(1,128)S(1)}, s32[1,2,1]{1,2,0:T(1,128)}, u32[]{:S(2)}) copy-start(s32[1,2,1]{1,2,0:T(1,128)} %param.20) | copy-start | bytes 28
  3.9 41.1 %copy-start.7 = (f32[1,2,1]{1,2,0:T(1,128)S(1)}, f32[1,2,1]{1,2,0:T(1,128)}, u32[]{:S(2)}) copy-start(f32[1,2,1]{1,2,0:T(1,128)} %param.21) | copy-start | bytes 28
  3.9 41.1 %copy-start.8 = (f32[128]{0:T(128)S(1)}, f32[128]{0:T(128)}, u32[]{:S(2)}) copy-start(f32[128]{0:T(128)} %param.17) | copy-start | bytes 1540
  44.9 1.1 copy-start.2
  46.0 1.1 copy-start.3
  47.1 1.1 copy-start.4
  48.2 1.1 copy-start.5
  108.6 2.5 %copy-start.9 = (f32[32,640]{1,0:T(8,128)S(1)}, f32[32,640]{1,0:T(8,128)}, u32[]{:S(2)}) copy-start(f32[32,640]{1,0:T(8,128)} %get-tuple-element.22) | copy-start | bytes 245764

commit v4 on v3

--- a/solution.py
+++ b/solution.py
@@ -379,7 +379,7 @@
 
 def sum_everywhere(blocks, bits):
     rows, columns = blocks.shape[-2:]
-    pieces_of = split_rows(rows, 4)
+    pieces_of = split_rows(rows, 2)
     count = len(pieces_of)
 
     def kernel(x_ref, o_ref, *scratch):

time: 112 us -> 111 us (level)
    pallas_call x1, Pallas kernels: 41 us -> 39.3 us  [sum_everywhere(): pl.pallas_call(kernel, out_shape=jax.ShapeDtypeStruct(blocks.shape, F32),...]
where the time goes in v4:
time: 111 us
  Pallas kernels  95.9 us (86%)
  local copies, waits for them, and re-layouts  10.8 us (10%)
  other arithmetic  3.23 us (3%)
    pallas_call x1, Pallas kernels, reduce_all(): pl.pallas_call(kernel, out_shape=(jax.ShapeDtypeStruct((rows, columns), F...  42.8 us
    pallas_call x1, Pallas kernels, sum_everywhere(): pl.pallas_call(kernel, out_shape=jax.ShapeDtypeStruct(blocks.shape, F32),...  39.3 us
    pallas_call x1, Pallas kernels, local_grads(): pl.pallas_call(functools.partial(mix_kernel, chunk=chunk), grid=(prompts,...  13.9 us
    unnamed x20, local copies, waits for them, and re-layouts  4.37 us
    select_n x1, other arithmetic, shards(): jnp.where(mine, local, 0.0).reshape(cube + (-1, width))  2.57 us
    slice x1, local copies, waits for them, and re-layouts, shards(): weight[:, :-8].reshape(gate_weight.shape)  2.5 us

profile of v4, /device:TPU:0, one launch (start us, length us, event | category | flops | bytes accessed | tf_op | source)
XLA Modules:
  0.0 110.7 jit_solution(14271023129058361572)
XLA Ops:
  0.6 0.7 compare_bitcast_fusion
  1.3 2.6 %broadcast_select_fusion.x_ref = f32[2,2,2,2,32,640]{5,4,3,2,1,0:T(8,128)} fusion(f32[2,2,2,2,32,640]{5,4,3,2,1,0:T(8,128)} %bitcast.46, pred[2]{0:T(512)(128)(4,1)S(1)} %compare_bitcast_fusion), kind=kLoop, calls=%fused_computation.1 | loop fusion | flops 327680 | bytes 2621442 | tf_op jit(solution)/shard_map/jit(_where)/select_n | solution.py:466
  3.9 0.0 copy-start
  3.9 0.0 copy-start.1
  3.9 0.0 copy-start.6
  3.9 0.0 copy-start.7
  3.9 0.0 copy-start.8
  3.9 39.3 %shard_map.162 = f32[2,2,2,2,32,640]{5,4,3,2,1,0:T(8,128)} custom-call(f32[2,2,2,2,32,640]{5,4,3,2,1,0:T(8,128)} %broadcast_select_fusion.x_ref), custom_call_target="tpu_custom_call" | custom-call | tf_op jit(solution)/shard_map/pallas_call | solution.py:398
  43.2 0.0 copy-done
  43.2 0.0 copy-done.1
  43.2 0.0 copy-done.6
  43.2 0.0 copy-done.7
  43.2 0.0 copy-done.8
  43.2 0.0 copy-start.2
  43.3 1.1 copy-done.2
  44.3 0.0 copy-start.3
  44.3 1.1 copy-done.3
  45.4 0.0 copy-start.4
  45.4 1.1 copy-done.4
  46.5 0.0 copy-start.5
  46.5 1.1 copy-done.5
  47.6 13.9 %shard_map.163 = (bf16[2,128,1280]{2,1,0:T(8,128)(2,1)}, bf16[2,128,1280]{2,1,0:T(8,128)(2,1)}, bf16[2,128,1280]{2,1,0:T(8,128)(2,1)}, bf16[2,128,2560]{2,1,0:T(...) custom-call(s32[2]{0:T(128)S(1)} %bitcast.39, f32[2]{0:T(128)S(1)} %bitcast.40, ...), custom_call_target="tpu_custom_call" | custom-call | tf_op jit(solution)/shard_map/pallas_call | solution.py:252
  61.5 0.4 reshape.49
  61.9 0.2 copy.24
  62.1 1.5 %reshape.50.s_ref = f32[2,2,2,2,32,640]{5,4,3,2,1,0:T(8,128)} reshape(f32[16,8,4,640]{3,2,1,0:T(4,128)S(1)} %bitcast.43) | data formatting | bytes 2621440 | tf_op jit(solution)/shard_map/reshape | solution.py:476
  63.6 42.8 %shard_map.164 = (f32[32,640]{1,0:T(8,128)}, f32[2,2,2,2,168,128]{5,4,3,2,1,0:T(8,128)}) custom-call(f32[2,2,2,2,32,640]{5,4,3,2,1,0:T(8,128)} %reshape.50.s_ref, f32[2,2,2,2,168,128]{5,4,3,2,1,0:T(8,128)} %bitcast.44), custom_call_target="tpu_custom_call" | custom-call | tf_op jit(solution)/shard_map/pallas_call | solution.py:439
  106.3 1.2 %slice_bitcast_fusion = f32[128]{0:T(128)} fusion(f32[16,168,128]{2,1,0:T(8,128)} %bitcast.47), kind=kLoop, calls=%fused_computation.3 | loop fusion | bytes 1024 | tf_op jit(solution)/shard_map/squeeze | solution.py:481
  107.5 0.0 copy-start.9
  107.5 2.5 %slice.8 = f32[16,160,128]{2,1,0:T(8,128)} slice(f32[16,168,128]{2,1,0:T(8,128)} %bitcast.48), slice={[0:16], [0:160], [0:128]} | slice | bytes 2621440 | tf_op jit(solution)/shard_map/slice | solution.py:481
  110.0 0.0 copy-done.9
  110.0 0.7 reshape.54
Async XLA Ops:
  3.9 39.3 %copy-start = (bf16[1,2,1,128,2560]{4,3,2,1,0:T(8,128)(2,1)S(1)}, bf16[1,2,1,128,2560]{4,3,2,1,0:T(8,128)(2,1)}, u32[]{:S(2)}) copy-start(bf16[1,2,1,128,2560]{4,3,2,1,0:T(8,128)(2,1)} %param.11) | copy-start | bytes 3932164
  3.9 39.3 %copy-start.1 = (bf16[1,2,1,128,1280]{4,3,2,1,0:T(8,128)(2,1)S(1)}, bf16[1,2,1,128,1280]{4,3,2,1,0:T(8,128)(2,1)}, u32[]{:S(2)}) copy-start(bf16[1,2,1,128,1280]{4,3,2,1,0:T(8,128)(2,1)} %param.12) | copy-start | bytes 1966084
  3.9 39.3 %copy-start.6 = (s32[1,2,1]{1,2,0:T(1,128)S(1)}, s32[1,2,1]{1,2,0:T(1,128)}, u32[]{:S(2)}) copy-start(s32[1,2,1]{1,2,0:T(1,128)} %param.20) | copy-start | bytes 28
  3.9 39.4 %copy-start.7 = (f32[1,2,1]{1,2,0:T(1,128)S(1)}, f32[1,2,1]{1,2,0:T(1,128)}, u32[]{:S(2)}) copy-start(f32[1,2,1]{1,2,0:T(1,128)} %param.21) | copy-start | bytes 28
  3.9 39.4 %copy-start.8 = (f32[128]{0:T(128)S(1)}, f32[128]{0:T(128)}, u32[]{:S(2)}) copy-start(f32[128]{0:T(128)} %param.17) | copy-start | bytes 1540
  43.2 1.1 copy-start.2
  44.3 1.1 copy-start.3
  45.4 1.1 copy-start.4
  46.5 1.1 copy-start.5
  107.5 2.5 %copy-start.9 = (f32[32,640]{1,0:T(8,128)S(1)}, f32[32,640]{1,0:T(8,128)}, u32[]{:S(2)}) copy-start(f32[32,640]{1,0:T(8,128)} %get-tuple-element.22) | copy-start | bytes 245764
